TPU v7x, 256 devices: a whole 4x4x8 slice. The times are simulated.
256 devices in a mesh: gx: 8 (over x, core), gy: 32 (over y, z).
Axes of the slice: x: 4, y: 4, z: 8, core: 2. Of those that a mesh axis runs over, the one named last changes fastest.
Arguments:
- tokens: bfloat16 [256, 8192], P('gy', 'gx'), may hold values from -6 to 6
- norm_gain: float32 [8192], P('gx'), may hold values from 0.5 to 1.5
- query_matrix: bfloat16 [8192, 8192], P('gx', 'gy'), may hold values from -0.0625 to 0.0625
- key_matrix: bfloat16 [8192, 1024], P('gx', 'gy'), may hold values from -0.0625 to 0.0625
- value_matrix: bfloat16 [8192, 1024], P('gx', 'gy'), may hold values from -0.0625 to 0.0625
- output_matrix: bfloat16 [8192, 8192], P('gx', 'gy'), may hold values from -0.0625 to 0.0625
- adapter_down: bfloat16 [64, 8192, 48], P('gy', 'gx'), may hold values from -0.0625 to 0.0625
- query_lift: bfloat16 [64, 16, 8192], P('gx', None, 'gy'), may hold values from -0.75 to 0.75
- key_value_lift: bfloat16 [64, 2, 16, 1024], P('gx', None, None, 'gy'), may hold values from -2.25 to 2.25
- mixer_down: bfloat16 [64, 8192, 16], P('gy', 'gx'), may hold values from -0.0625 to 0.0625
- mixer_lift: bfloat16 [64, 16, 8192], P('gx', None, 'gy'), may hold values from -0.75 to 0.75
- adapter_index: int32 [256], replicated, may hold values from 0 to 63
- suffix_lengths: int32 [256], P(('gx', 'gy')), may hold values from 1 to 2048, 262144 in all
- shared_prefix_keys: bfloat16 [16384, 1024], P('gy'), may hold values from -1000 to 1000
- shared_prefix_values: bfloat16 [16384, 1024], P('gy'), may hold values from -6 to 6
- private_suffix_keys: bfloat16 [256, 2048, 1024], P(('gx', 'gy')), may hold values from -40 to 40
- private_suffix_values: bfloat16 [256, 2048, 1024], P(('gx', 'gy')), may hold values from -6 to 6
Outputs:
- output: bfloat16 [256, 8192], P(('gx', 'gy'))
Inputs may be any that keep to these rules, and one draw needn't show every extreme that they name: `adapter_index`: each agent's adapter. `suffix_lengths`: the agents' lengths add up to 262144, and some agent has exactly 2048.
All inputs are finite; a program needn't handle non-finite values. No bound on the sum of `suffix_lengths` on one device may be relied on, other than what follows from the above.
Results may differ from a plain program's by a relative error of at most 0.024.
Values may be sent and summed in bfloat16 or wider, within the bound.
A program may use at most 64 MiB of HBM per device.

v0:
```python
import math

import jax
import jax.numpy as jnp
from jax import lax
from jax.sharding import PartitionSpec as P

MODEL_WIDTH = 8192
QUERY_HEADS = 64
KEY_HEADS = 8
HEAD_SIZE = 128
PREFIX_LENGTH = 16384


EPSILON = 1e-05
ADAPTER_SCALE = 2.0
ROPE_BASE = 500000.0


def apply_rotary(vectors, token_position):
    half_dim = vectors.shape[-1] // 2
    steps = jnp.arange(half_dim).astype(jnp.float32)
    frequency = jnp.power(jnp.float32(ROPE_BASE), -2.0 * steps / vectors.shape[-1])
    angles = token_position[..., None] * frequency
    cosine = jnp.cos(angles)
    sine_part = jnp.sin(angles)
    front_half = vectors[..., :half_dim]
    back_half = vectors[..., half_dim:]
    return jnp.concatenate(
        [front_half * cosine - back_half * sine_part, back_half * cosine + front_half * sine_part],
        axis=-1,
    )


def spread_token_rows(adapter_update, owners, slots_here):
    selected = (owners[:, None] == jnp.arange(slots_here)[None, :]).astype(adapter_update.dtype)
    return (selected[:, :, None] * adapter_update[:, None, :]).reshape(
        adapter_update.shape[0], slots_here * adapter_update.shape[1]
    )


def local(
    tokens,
    norm_gain,
    query_matrix,
    key_matrix,
    value_matrix,
    output_matrix,
    adapter_down,
    query_lift,
    key_value_lift,
    mixer_down,
    mixer_lift,
    adapter_index,
    suffix_lengths,
    shared_prefix_keys,
    shared_prefix_values,
    private_suffix_keys,
    private_suffix_values,
):
    gx_count = lax.axis_size("gx")
    column_groups = lax.axis_size("gy")
    gx_place = lax.axis_index("gx")
    gy_place = lax.axis_index("gy")
    gathered = lax.all_gather(tokens, "gy", axis=0, tiled=True)
    tokens_f = gathered.astype(jnp.float32)
    squares = jnp.sum(tokens_f * tokens_f, axis=1)
    scaled_scores = (tokens_f * norm_gain[None, :]).astype(jnp.bfloat16)
    down_here = adapter_down.shape[0]
    lift_here = query_lift.shape[0]
    rank_size = query_lift.shape[1]
    down_owner = adapter_index - gy_place * down_here
    lift_owner = adapter_index - gx_place * lift_here
    picked = (down_owner[:, None] == jnp.arange(down_here)[None, :]).astype(jnp.float32)
    down_terms = jnp.einsum(
        "ad,edr->aer", scaled_scores, adapter_down, preferred_element_type=jnp.float32
    )
    down_part = jnp.sum(down_terms * picked[:, :, None], axis=1)
    adapter_update = lax.psum(down_part, ("gx", "gy")).astype(jnp.bfloat16)
    query_columns = query_matrix.shape[1]
    paired_columns = key_matrix.shape[1]
    query_lifted = jnp.dot(
        spread_token_rows(adapter_update[:, :rank_size], lift_owner, lift_here),
        query_lift.reshape(lift_here * rank_size, query_columns),
        preferred_element_type=jnp.float32,
    )
    key_lifted = jnp.dot(
        spread_token_rows(adapter_update[:, rank_size : 2 * rank_size], lift_owner, lift_here),
        key_value_lift[:, 0].reshape(lift_here * rank_size, paired_columns),
        preferred_element_type=jnp.float32,
    )
    value_lifted = jnp.dot(
        spread_token_rows(adapter_update[:, 2 * rank_size :], lift_owner, lift_here),
        key_value_lift[:, 1].reshape(lift_here * rank_size, paired_columns),
        preferred_element_type=jnp.float32,
    )
    partial_value = jnp.concatenate(
        [
            jnp.dot(scaled_scores, query_matrix, preferred_element_type=jnp.float32)
            + ADAPTER_SCALE * query_lifted,
            jnp.dot(scaled_scores, key_matrix, preferred_element_type=jnp.float32)
            + ADAPTER_SCALE * key_lifted,
            jnp.dot(scaled_scores, value_matrix, preferred_element_type=jnp.float32)
            + ADAPTER_SCALE * value_lifted,
        ],
        axis=1,
    )
    width_all = partial_value.shape[1]
    summed, summed_squares = (
        lax.psum_scatter(partial_value, "gx", scatter_dimension=0, tiled=True),
        lax.psum_scatter(squares, "gx", scatter_dimension=0, tiled=True),
    )
    own_squares = lax.dynamic_slice_in_dim(summed_squares, gy_place, 1, 0)
    agent_columns = lax.all_to_all(summed, "gy", split_axis=0, concat_axis=1, tiled=True)
    agent_columns = agent_columns.reshape(column_groups, width_all)
    agent_factor = lax.rsqrt(own_squares.reshape(()) / MODEL_WIDTH + EPSILON)
    token_position = (PREFIX_LENGTH + suffix_lengths).astype(jnp.float32)
    query_vectors = apply_rotary(
        (agent_columns[:, :query_columns] * agent_factor).reshape(QUERY_HEADS, HEAD_SIZE),
        token_position,
    ).astype(jnp.bfloat16)
    fresh_keys = apply_rotary(
        (agent_columns[:, query_columns : query_columns + paired_columns] * agent_factor).reshape(
            KEY_HEADS, HEAD_SIZE
        ),
        token_position,
    ).astype(jnp.bfloat16)
    fresh_values = (
        (agent_columns[:, query_columns + paired_columns :] * agent_factor)
        .reshape(KEY_HEADS, HEAD_SIZE)
        .astype(jnp.bfloat16)
    )
    heads_per_group = QUERY_HEADS // KEY_HEADS
    inv_root = 1.0 / math.sqrt(HEAD_SIZE)
    gathered_queries = lax.all_gather(
        query_vectors.reshape(1, QUERY_HEADS * HEAD_SIZE), "gy", axis=0, tiled=True
    ).reshape(column_groups, KEY_HEADS, heads_per_group, HEAD_SIZE)
    prefix_key_rows = shared_prefix_keys.reshape(-1, KEY_HEADS, HEAD_SIZE)
    prefix_value_rows = shared_prefix_values.reshape(-1, KEY_HEADS, HEAD_SIZE)
    scores = (
        jnp.einsum(
            "akgd,pkd->akgp", gathered_queries, prefix_key_rows, preferred_element_type=jnp.float32
        )
        * inv_root
    )
    peak = jnp.max(scores, axis=-1)
    weights = jnp.exp(scores - peak[..., None])
    mass = jnp.sum(weights, axis=-1)
    partial_sum = jnp.einsum(
        "akgp,pkd->akgd",
        weights.astype(jnp.bfloat16),
        prefix_value_rows,
        preferred_element_type=jnp.float32,
    )
    peak_all = lax.pmax(peak, "gy")
    shrink = jnp.exp(peak - peak_all)
    own_sum, own_mass = (
        lax.psum_scatter(partial_sum * shrink[..., None], "gy", scatter_dimension=0, tiled=True),
        lax.psum_scatter(mass * shrink, "gy", scatter_dimension=0, tiled=True),
    )
    run_peak = lax.dynamic_slice_in_dim(peak_all, gy_place, 1, 0)[0]
    run_mass = own_mass[0]
    run_sum = own_sum[0]
    agent_query = query_vectors.reshape(KEY_HEADS, heads_per_group, HEAD_SIZE)
    own_length = suffix_lengths[0]
    suffix_span = private_suffix_keys.shape[1]
    block_length = min(512, suffix_span)
    block_total = (own_length + block_length - 1) // block_length
    agent_keys = private_suffix_keys[0]
    agent_values = private_suffix_values[0]

    def visit(block_index, running):
        old_peak, old_mass, old_sum = running
        offset = block_index * block_length
        key_block = lax.dynamic_slice_in_dim(agent_keys, offset, block_length, 0).reshape(
            block_length, KEY_HEADS, HEAD_SIZE
        )
        value_block = lax.dynamic_slice_in_dim(agent_values, offset, block_length, 0).reshape(
            block_length, KEY_HEADS, HEAD_SIZE
        )
        block_scores = (
            jnp.einsum("kgd,pkd->kgp", agent_query, key_block, preferred_element_type=jnp.float32)
            * inv_root
        )
        live_mask = offset + jnp.arange(block_length) < own_length
        block_scores = jnp.where(live_mask[None, None, :], block_scores, -jnp.inf)
        new_peak = jnp.maximum(old_peak, jnp.max(block_scores, axis=-1))
        decay_factor = jnp.exp(old_peak - new_peak)
        block_weights = jnp.exp(block_scores - new_peak[..., None])
        next_mass = old_mass * decay_factor + jnp.sum(block_weights, axis=-1)
        next_sum = old_sum * decay_factor[..., None] + jnp.einsum(
            "kgp,pkd->kgd",
            block_weights.astype(jnp.bfloat16),
            value_block,
            preferred_element_type=jnp.float32,
        )
        return (new_peak, next_mass, next_sum)

    run_peak, run_mass, run_sum = lax.fori_loop(
        0, block_total, visit, (run_peak, run_mass, run_sum)
    )
    new_scores = (
        jnp.sum(
            agent_query.astype(jnp.float32) * fresh_keys.astype(jnp.float32)[:, None, :], axis=-1
        )
        * inv_root
    )
    final_peak = jnp.maximum(run_peak, new_scores)
    final_shrink = jnp.exp(run_peak - final_peak)
    new_weight = jnp.exp(new_scores - final_peak)
    new_rounded = lax.optimization_barrier(new_weight.astype(jnp.bfloat16)).astype(jnp.float32)
    final_mass = run_mass * final_shrink + new_weight
    final_sum = (
        run_sum * final_shrink[..., None]
        + new_rounded[..., None] * fresh_values.astype(jnp.float32)[:, None, :]
    )
    decode_attention = (
        (final_sum / final_mass[..., None]).reshape(1, QUERY_HEADS * HEAD_SIZE).astype(jnp.bfloat16)
    )
    head_blocks = lax.all_to_all(decode_attention, "gx", split_axis=1, concat_axis=0, tiled=True)
    block_width = head_blocks.shape[1]
    attention_rows = lax.all_gather(
        head_blocks.reshape(gx_count, 1, block_width), "gy", axis=1, tiled=True
    ).reshape(gx_count * column_groups, block_width)
    mixer_terms = jnp.einsum(
        "aw,ewr->aer", attention_rows, mixer_down, preferred_element_type=jnp.float32
    )
    mixer_part = jnp.sum(mixer_terms * picked[:, :, None], axis=1)
    lowmix = lax.psum(mixer_part, ("gx", "gy")).astype(jnp.bfloat16)
    out_cols = output_matrix.shape[1]
    output_lifted = jnp.dot(
        spread_token_rows(lowmix, lift_owner, lift_here),
        mixer_lift.reshape(lift_here * rank_size, out_cols),
        preferred_element_type=jnp.float32,
    )
    output_part = (
        jnp.dot(attention_rows, output_matrix, preferred_element_type=jnp.float32)
        + ADAPTER_SCALE * output_lifted
    )
    output_summed = lax.psum_scatter(output_part, "gx", scatter_dimension=0, tiled=True)
    return lax.all_to_all(
        output_summed.astype(jnp.bfloat16), "gy", split_axis=0, concat_axis=1, tiled=True
    )


def solution(mesh):
    return jax.shard_map(
        local,
        mesh=mesh,
        in_specs=(
            P("gy", "gx"),
            P("gx"),
            P("gx", "gy"),
            P("gx", "gy"),
            P("gx", "gy"),
            P("gx", "gy"),
            P("gy", "gx", None),
            P("gx", None, "gy"),
            P("gx", None, None, "gy"),
            P("gy", "gx", None),
            P("gx", None, "gy"),
            P(),
            P(("gx", "gy")),
            P("gy", None),
            P("gy", None),
            P(("gx", "gy"), None, None),
            P(("gx", "gy"), None, None),
        ),
        out_specs=P(("gx", "gy"), None),
        check_vma=False,
    )
```

profile of v0, /device:TPU:1, one launch (start us, length us, event | category | flops | bytes accessed | tf_op | source)
XLA Modules:
  0.0 743.6 jit_solution(2365501339443797621)
XLA Ops:
  8.1 42.3 %all_gather.9 = bf16[256,1024]{1,0:T(8,128)(2,1)S(1)} all-gather(bf16[8,1024]{1,0:T(8,128)(2,1)} %param.19), channel_id=1, replica_groups=mesh['gx'=8,'gy'=32] {'gy'}, dimensions={0}, use_global_device_ids=true | all-gather | bytes 540672 | tf_op jit(solution)/shard_map/all_gather | solution.py:65
  53.9 86.3 %psum.14 = bf16[256,48]{0,1:T(8,128)(2,1)S(1)} all-reduce(f32[256,48]{0,1:T(8,128)S(1)} %multiply_reduce_fusion), channel_id=1, replica_groups=mesh['gx'=8,'gy'=32] {'gx','gy'}, use_global_device_ids=true, to_apply=%region_1.0 | all-reduce | flops 12288 | bytes 73728 | tf_op jit(solution)/shard_map/psum | solution.py:79
  145.8 12.7 %all-reduce = f32[256]{0:T(256)S(1)} all-reduce(f32[256]{0:T(256)S(1)} %fusion.24), channel_id=4, replica_groups=mesh['gx'=8,'gy'=32] {'gx'}, use_global_device_ids=true, to_apply=%region_4.0.clone | all-reduce | flops 256 | bytes 2048
  161.3 2.5 copy.87
  163.8 6.4 reduce-scatter.8.cloned.1.call-done
  171.9 9.2 %all-to-all-start = ((f32[32,1,320]{2,1,0:T(1,128)}), f32[32,1,320]{2,1,0:T(1,128)S(1)}, u32[]{:S(2)}, u32[]{:S(2)}) async-start(f32[32,1,320]{2,1,0:T(1,128)} %copy.56), calls=%async_computation | async-start | bytes 98304 | tf_op jit(solution)/shard_map/all_to_all | solution.py:114
  181.2 8.7 %all-to-all-done = f32[32,1,320]{2,1,0:T(1,128)S(1)} async-done(((f32[32,1,320]{2,1,0:T(1,128)}), f32[32,1,320]{2,1,0:T(1,128)S(1)}, u32[]{:S(2)}, u32[]{:S(2)}) %all-to-all-start) | async-done | bytes 40992 | tf_op jit(solution)/shard_map/all_to_all | solution.py:114
  190.1 36.6 %all-gather.1 = bf16[32,1,8192]{2,1,0:T(2,128)(2,1)S(1)} all-gather(bf16[1,1,8192]{2,1,0:T(2,128)(2,1)S(1)} %reshape.229), channel_id=1, replica_groups=mesh['gx'=8,'gy'=32] {'gy'}, dimensions={0}, use_global_device_ids=true | all-gather | bytes 540672 | tf_op jit(solution)/shard_map/all_gather | solution.py:135
  226.7 3.2 reduce
  230.0 2.7 bitcast_reduce_fusion
  232.7 112.6 %pmax.7 = f32[32,8,8]{2,0,1:T(8,128)S(1)} all-reduce(f32[32,8,8]{2,0,1:T(8,128)S(1)} %get-tuple-element.104), channel_id=1, replica_groups=mesh['gx'=8,'gy'=32] {'gy'}, use_global_device_ids=true, to_apply=%region_6.0 | all-reduce | flops 2048 | bytes 16384 | tf_op jit(solution)/shard_map/pmax | solution.py:155
  345.2 3.4 fusion.8
  348.7 2.1 fusion.16
  351.7 6.5 copy.61
  358.2 6.5 copy.62
  365.0 110.6 %all-reduce.1 = f32[32,8,8]{2,1,0:T(8,128)S(1)} all-reduce(f32[32,8,8]{2,1,0:T(8,128)S(1)} %copy.59), channel_id=5, replica_groups=mesh['gx'=8,'gy'=32] {'gy'}, use_global_device_ids=true, to_apply=%region_8.0.clone | all-reduce | flops 2048 | bytes 16384
  476.6 53.6 %all-reduce.5.cloned.1.call-done = f32[32,8,8,128]{3,2,0,1:T(8,128)} async-done(((f32[32,8,8,128]{3,2,0,1:T(8,128)}), f32[32,8,8,128]{3,2,0,1:T(8,128)}) %all-reduce.5.cloned.1.call-update) | async-done | bytes 1048592
  531.6 6.6 while.14
  539.7 30.1 %all_to_all.42 = bf16[8,2,512]{2,1,0:T(2,128)(2,1)S(1)} all-to-all(bf16[8,2,512]{2,1,0:T(2,128)(2,1)S(1)} %reshape.252), channel_id=1, replica_groups=mesh['gx'=8,'gy'=32] {'gx'}, dimensions={0} | all-to-all | bytes 32768 | tf_op jit(solution)/shard_map/all_to_all | solution.py:220
  569.8 34.2 %all-gather = bf16[1,8,32768]{2,0,1:T(2,128)(2,1)S(1)} all-gather(bf16[1,8,1024]{2,0,1:T(2,128)(2,1)S(1)} %bitcast.128), channel_id=2, replica_groups=mesh['gx'=8,'gy'=32] {'gy'}, dimensions={2}, use_global_device_ids=true | all-gather | bytes 540672 | tf_op jit(solution)/shard_map/all_gather | solution.py:222
  604.0 3.2 reduce.1
  607.7 82.2 %psum.15 = bf16[256,16]{0,1:T(8,128)(2,1)S(1)} all-reduce(f32[256,16]{0,1:T(8,128)S(1)} %multiply_reduce_fusion.1), channel_id=1, replica_groups=mesh['gx'=8,'gy'=32] {'gx','gy'}, use_global_device_ids=true, to_apply=%region_16.17 | all-reduce | flops 4096 | bytes 24576 | tf_op jit(solution)/shard_map/psum | solution.py:229
  691.4 25.6 %reduce-scatter.10.cloned.1.call-done = f32[32,256]{1,0:T(8,128)} async-done(((f32[256,256]{1,0:T(8,128)}), f32[32,256]{1,0:T(8,128)}) %reduce-scatter.10.cloned.1.call-update) | async-done | bytes 32784
  718.7 17.7 %all_to_all.43 = bf16[32,2,128]{2,1,0:T(2,128)(2,1)S(1)} all-to-all(bf16[32,2,128]{2,1,0:T(2,128)(2,1)S(1)} %reshape.254), channel_id=1, replica_groups=mesh['gx'=8,'gy'=32] {'gy'}, dimensions={0} | all-to-all | bytes 32768 | tf_op jit(solution)/shard_map/all_to_all | solution.py:241
  (99 shorter events, 29.2 us)
Async XLA Ops:
  6.5 134.8 %copy-start = (bf16[1024,256]{1,0:T(8,128)(2,1)S(1)}, bf16[1024,256]{1,0:T(8,128)(2,1)}, u32[]{:S(2)}) copy-start(bf16[1024,256]{1,0:T(8,128)(2,1)} %param.21) | copy-start | bytes 1572868
  6.5 137.8 %copy-start.7 = (u32[256]{0:T(256)S(1)}, u32[256]{0:T(256)}, u32[]{:S(2)}) copy-start(u32[256]{0:T(256)} %constant.84) | copy-start | bytes 3076
  6.5 163.7 %reduce-scatter.8.cloned.1.call-start = ((), (), s32[]{:S(2)}) async-start(), calls=%async_computation.5 | async-start | bytes 442368
  171.9 18.1 %all-to-all-start = ((f32[32,1,320]{2,1,0:T(1,128)}), f32[32,1,320]{2,1,0:T(1,128)S(1)}, u32[]{:S(2)}, u32[]{:S(2)}) async-start(f32[32,1,320]{2,1,0:T(1,128)} %copy.56), calls=%async_computation | async-start | bytes 98304 | tf_op jit(solution)/shard_map/all_to_all | solution.py:114
  181.1 349.1 %all-reduce.5.cloned.1.call-start = ((), (), s32[]{:S(2)}) async-start(), calls=%async_computation.7 | async-start | bytes 2097152
  232.7 116.0 %copy-start.2 = (bf16[64,8,8,128]{3,2,1,0:T(8,128)(2,1)S(1)}, bf16[64,8,8,128]{3,2,1,0:T(8,128)(2,1)}, u32[]{:S(2)}) copy-start(bf16[64,8,8,128]{3,2,1,0:T(8,128)(2,1)} %copy.87) | copy-start | bytes 3145732
  345.2 3.4 copy-start.1
  348.6 2.4 copy-start.6
  350.8 366.3 %reduce-scatter.10.cloned.1.call-start = ((), (), s32[]{:S(2)}) async-start(), calls=%async_computation.6 | async-start | bytes 294912
  531.6 75.8 %copy-start.4 = (bf16[2,1024,16]{1,2,0:T(8,128)(2,1)S(1)}, bf16[2,1024,16]{1,2,0:T(8,128)(2,1)}, u32[]{:S(2)}) copy-start(bf16[2,1024,16]{1,2,0:T(8,128)(2,1)} %param.28) | copy-start | bytes 196612
  538.3 151.7 %copy-start.5 = (bf16[8,16,256]{2,1,0:T(8,128)(2,1)S(1)}, bf16[8,16,256]{2,1,0:T(8,128)(2,1)}, u32[]{:S(2)}) copy-start(bf16[8,16,256]{2,1,0:T(8,128)(2,1)} %param.29) | copy-start | bytes 196612
  538.3 151.9 %copy-start.3 = (bf16[1024,256]{1,0:T(8,128)(2,1)S(1)}, bf16[1024,256]{1,0:T(8,128)(2,1)}, u32[]{:S(2)}) copy-start(bf16[1024,256]{1,0:T(8,128)(2,1)} %param.24) | copy-start | bytes 1572868
Sparse Core Ops, SparseCore 0:
  143.8 26.3 reduce-scatter.7
  350.9 179.2 all-reduce.4
  691.6 25.4 reduce-scatter.9
where the time goes:
time: 748 us; the launch traced here: 744 us
  blocking collectives  565 us (76%)
  waiting for transfers between devices  94.4 us (13%)
  local copies, waits for them, and re-layouts  31.3 us (4%)
  between operations  15.5 us (2%)
  other arithmetic  14.6 us (2%)
  matrix products  13 us (2%)
  starting transfers between devices  9.51 us (1%)
    unnamed x2, blocking collectives  123 us
    pmax x1, blocking collectives, local(): peak_all = lax.pmax(peak, 'gy')  113 us
    psum x1, blocking collectives, local(): adapter_update = lax.psum(down_part, ('gx', 'gy')).astype(jnp.bfloat16)  86.3 us
    unnamed x6, waiting for transfers between devices  85.7 us
    psum x1, blocking collectives, local(): lowmix = lax.psum(mixer_part, ('gx', 'gy')).astype(jnp.bfloat16)  82.2 us
    all_gather x1, blocking collectives, local(): gathered = lax.all_gather(tokens, 'gy', axis=0, tiled=True)  42.3 us
    all_gather x1, blocking collectives, local(): lax.all_gather(query_vectors.reshape(1, QUERY_HEADS * HEAD_SIZE), 'gy', a...  36.6 us
    all_gather x1, blocking collectives, local(): lax.all_gather(head_blocks.reshape(gx_count, 1, block_width), 'gy', axis=...  34.2 us
  transfers between devices with their start and end apart: 4, of which 4 were waited for; matrix products, arithmetic and copies ran while one was open for 3% of the time, Pallas kernels for 0%

commit v1 on v0

v1 whole, which is shorter than its diff:
```python
import math

import jax
import jax.numpy as jnp
from jax import lax
from jax.experimental import pallas as pl
from jax.experimental.pallas import tpu as pltpu
from jax.sharding import PartitionSpec as P

MODEL_WIDTH = 8192
HEAD_SIZE = 128
PREFIX_LENGTH = 16384
EPSILON = 1e-05
ADAPTER_SCALE = 2.0
ROPE_BASE = 500000.0
RANK = 16

MESH = pl.DeviceIdType.MESH
F32 = jnp.float32
BF16 = jnp.bfloat16
NEG = -1e30


def iota(shape, dim):
    return lax.broadcasted_iota(jnp.int32, shape, dim)


def one_hot(cond):
    return jnp.where(cond, 1.0, 0.0).astype(BF16)


def dot(a, b):
    return jnp.dot(a, b, preferred_element_type=F32)


def dot_t(a, b):
    return lax.dot_general(a, b, (((1,), (1,)), ((), ())), preferred_element_type=F32)


class Net:
    def __init__(self, gx_count, gy_count):
        self.nx, self.ny = gx_count, gy_count
        self.gx, self.gy = lax.axis_index("gx"), lax.axis_index("gy")

    def along(self, axis):
        if axis == "gy":
            return self.gy, self.ny, lambda p: (self.gx, p)
        return self.gx, self.nx, lambda p: (p, self.gy)

    def barrier(self, axes):
        sem = pltpu.get_barrier_semaphore()
        total = 0
        for axis in axes:
            me, n, dev = self.along(axis)
            total += n - 1

            def one(s, c):
                pl.semaphore_signal(sem, inc=1, device_id=dev(lax.rem(me + s, n)), device_id_type=MESH)
                return c

            lax.fori_loop(1, n, one, 0)
        pl.semaphore_wait(sem, total)

    def exchange(self, axis, src_at, dst, slot, ssem, rsem):
        me, n, dev = self.along(axis)

        def copy(peer, target):
            return pltpu.make_async_remote_copy(
                src_ref=src_at(peer), dst_ref=dst.at[slot(target)],
                send_sem=ssem.at[peer], recv_sem=rsem.at[target],
                device_id=dev(peer), device_id_type=MESH)

        def start():
            def one(s, c):
                copy(lax.rem(me + s, n), me).start()
                return c
            lax.fori_loop(1, n, one, 0)

        def wait_recv():
            def one(s, c):
                peer = lax.rem(me + n - s, n)
                copy(peer, peer).wait_recv()
                return c
            lax.fori_loop(1, n, one, 0)

        def wait_send():
            def one(s, c):
                copy(lax.rem(me + s, n), me).wait_send()
                return c
            lax.fori_loop(1, n, one, 0)

        return start, wait_recv, wait_send

    def gather(self, axis, buf, ssem, rsem):
        me, _, _ = self.along(axis)
        return self.exchange(axis, lambda p: buf.at[me], buf, lambda i: i, ssem, rsem)

    def scatter(self, axis, src, dst, ssem, rsem):
        return self.exchange(axis, lambda p: src.at[p], dst, lambda i: i, ssem, rsem)


def index_columns(idx_ref):
    count = idx_ref.shape[1]
    row = jnp.broadcast_to(idx_ref[...].astype(F32), (count, count))
    diagonal = iota((count, count), 0) == iota((count, count), 1)
    return jnp.sum(jnp.where(diagonal, row, 0.0), axis=1, keepdims=True)


def spread(low, pattern, adapter_column):
    wide = dot(low, pattern)
    owner = (iota(wide.shape, 1) // RANK).astype(F32)
    return jnp.where(owner == adapter_column, wide, 0.0).astype(BF16)


def project_body(net, r, q_out, kv_out):
    nx, ny, gx, gy = net.nx, net.ny, net.gx, net.gy
    agents = nx * ny
    tok, lift = r["tok"], r["lift"]
    tok[gy, :, 0:1024] = r["tokens"][...]
    cs = jnp.broadcast_to(r["cs"][...], (nx, 128))
    high = cs.astype(BF16).astype(F32)
    mid = (cs - high).astype(BF16).astype(F32)
    row = iota((nx, 128), 0)
    if nx >= 3:
        low3 = cs - high - mid
        parts = jnp.where(row == 0, high, jnp.where(row == 1, mid, jnp.where(row == 2, low3, 0.0)))
    else:
        parts = jnp.where(row == 0, high, mid)
    tok[gy, :, 1024:1152] = parts.astype(BF16)
    lift[gx] = r["lift_in"][...]
    t_start, t_recv, t_send = net.gather("gy", tok, r["tok_s"], r["tok_r"])
    l_start, l_recv, l_send = net.gather("gx", lift, r["lift_s"], r["lift_r"])
    t_start()
    l_start()
    adapters = index_columns(r["idx"])
    r["cols"][...] = jnp.broadcast_to(adapters, (agents, 128))
    t_recv()
    x = tok[:, :, 0:1024].astype(F32).reshape(agents, 1024)
    squares = jnp.sum(x * x, axis=1, keepdims=True)
    scaled = (x * r["gain"][...]).astype(BF16)
    first = dot(scaled, r["wcat"][...])
    lane = iota((agents, 128), 1)
    base = (gy * 2).astype(F32)
    down = jnp.where(adapters == base, first[:, 0:128],
                     jnp.where(adapters == base + 1.0, first[:, 128:256], 0.0))
    down = jnp.where(lane < 3 * RANK, down, jnp.where(lane == 127, squares, 0.0))
    rows = agents // nx
    r["rl_src"][...] = down.reshape(nx, rows, 128)
    r["rl"][gx] = r["rl_src"][gx]
    rl_start, rl_recv, rl_send = net.scatter("gx", r["rl_src"], r["rl"], r["rl_s"], r["rl_r"])
    rl_start()
    r["rm_src"][:, :, 256:384] = first[:, 0:128].reshape(nx, rows, 128)
    r["rm_src"][:, :, 0:256] = dot(scaled, r["wq"][...]).reshape(nx, rows, 256)
    r["rm"][gx] = r["rm_src"][gx]
    rm_start, rm_recv, rm_send = net.scatter("gx", r["rm_src"], r["rm"], r["rm_s"], r["rm_r"])
    rm_start()
    rl_recv()
    low = jnp.sum(r["rl"][...], axis=0)
    factor = lax.rsqrt(low[:, 127:128] / (nx * 1024) + EPSILON)
    al = r["al"]
    al[gy] = jnp.where(iota((rows, 128), 1) < 3 * RANK, low, 0.0).astype(BF16)
    al_start, al_recv, al_send = net.gather("gy", al, r["al_s"], r["al_r"])
    al_start()
    width = nx * 128
    pattern_row, pattern_rank = iota((128, width), 0), iota((128, width), 1) & (RANK - 1)
    patterns = [one_hot(pattern_row == pattern_rank + part * RANK) for part in range(3)]
    ctab = jnp.sum(tok[:, :, 1024:1152].astype(F32), axis=1)
    turned = pltpu.roll(ctab, 64, 1)
    front = iota(ctab.shape, 1) < 64
    cosines = jnp.where(front, ctab, turned)
    sines = jnp.where(front, -turned, ctab)
    own_adapter = r["cols"][pl.ds(pl.multiple_of(gx * rows, 8), rows), 0:1]
    rm_recv()
    summed = jnp.sum(r["rm"][...], axis=0)
    l_recv()
    lift_all = lift[...].reshape(width, 384)
    al_recv()
    lowrank = jnp.sum(al[...].astype(F32), axis=0).astype(BF16)
    q_up = dot(spread(lowrank, patterns[0], own_adapter), lift_all[:, 0:256])
    k_up = dot(spread(lowrank, patterns[1], own_adapter), lift_all[:, 256:384])
    v_up = dot(spread(lowrank, patterns[2], own_adapter), lift_all[:, 256:384])
    q = (summed[:, 0:256] + ADAPTER_SCALE * q_up) * factor
    kv_up = jnp.where(iota((rows, 128), 1) < 96, k_up, v_up)
    kv_out[...] = (summed[:, 256:384] + ADAPTER_SCALE * kv_up) * factor
    for t in range(2):
        u = q[:, t * 128:(t + 1) * 128]
        q_out[:, t * 128:(t + 1) * 128] = (u * cosines + pltpu.roll(u, 64, 1) * sines).astype(BF16)
    return [t_send, l_send, rl_send, rm_send, al_send]


def attend_body(net, r, q_in, kv_in, att_out):
    nx, ny, gx, gy = net.nx, net.ny, net.gx, net.gy
    rows = ny
    kv_heads = nx
    parts = ny // kv_heads
    inv_root = 1.0 / math.sqrt(HEAD_SIZE)
    qbuf, kvs, kvb, osend, obuf, qp = r["qbuf"], r["kvs"], r["kvb"], r["osend"], r["obuf"], r["qp"]
    qbuf[gy] = q_in[...]
    q_start, q_recv, q_send = net.gather("gy", qbuf, r["q_s"], r["q_r"])
    q_start()
    for i in range(rows):
        kvs[i] = kv_in[i:i + 1, :]

    def place(i):
        return lax.rem(i, parts) * kv_heads + i // parts

    kvb[place(gy)] = kvs[gy]
    k_start, k_recv, k_send = net.exchange("gy", lambda p: kvs.at[p], kvb, place, r["kv_s"], r["kv_r"])
    k_start()
    count = rows * 8
    target, source = iota((count, count), 0), iota((count, count), 1)
    perm = one_hot(source == (target & 7) * rows + (target >> 3))
    lane3 = iota((rows, 8, 128), 2)
    stats = jnp.zeros((rows, 8, 128), F32)
    q_recv()
    for h in range(kv_heads):
        blocks = [qbuf[h * parts + j, :, t * 128:(t + 1) * 128] for j in range(parts) for t in range(2)]
        qh = dot(perm, jnp.concatenate(blocks, axis=0))
        qp[h] = qh.reshape(rows, 8, 128)
        scores = dot_t(qh.astype(BF16), r["pk"][:, h * 128:(h + 1) * 128]) * inv_root
        peak = jnp.max(scores, axis=1, keepdims=True)
        weights = jnp.exp(scores - peak)
        mass = jnp.sum(weights, axis=1, keepdims=True)
        out = dot(weights.astype(BF16), r["pv"][:, h * 128:(h + 1) * 128]) / mass
        osend[h] = out.reshape(rows, 8, 128).astype(BF16)
        here = (lane3 & 7) == h
        stats = jnp.where(here & (lane3 < 24), peak.reshape(rows, 8, 1), stats)
        stats = jnp.where(here & (lane3 >= 24) & (lane3 < 48), mass.reshape(rows, 8, 1), stats)
    high = stats.astype(BF16).astype(F32)
    mid = (stats - high).astype(BF16).astype(F32)
    low = stats - high - mid
    third = (lane3 >> 3)
    third = jnp.where(third >= 3, third - 3, third)
    coded = jnp.where(third == 0, high, jnp.where(third == 1, mid, low))
    osend[kv_heads] = jnp.where(lane3 < 48, coded, 0.0).astype(BF16)
    for h in range(kv_heads + 1):
        obuf[gy, h] = osend[h, gy]
    o_start, o_recv, o_send = net.exchange(
        "gy", lambda p: osend.at[:, p], obuf, lambda i: i, r["o_s"], r["o_r"])
    o_start()
    span = r["sk"].shape[1]
    live = iota((8, span), 1) < r["len"][0]
    lane = iota((8, 128), 1)
    own_peak = jnp.zeros((8, 128), F32)
    own_mass = jnp.zeros((8, 128), F32)
    own_out = []
    for h in range(kv_heads):
        qh = qp[h, gy].astype(BF16)
        scores = dot_t(qh, r["sk"][0, :, h * 128:(h + 1) * 128]) * inv_root
        scores = jnp.where(live, scores, NEG)
        peak = jnp.max(scores, axis=1, keepdims=True)
        weights = jnp.exp(scores - peak)
        mass = jnp.sum(weights, axis=1, keepdims=True)
        own_out.append(dot(weights.astype(BF16), r["sv"][0, :, h * 128:(h + 1) * 128]) / mass)
        own_peak = jnp.where(lane == h, peak, own_peak)
        own_mass = jnp.where(lane == h, mass, own_mass)
    k_recv()
    head_row = iota((kv_heads, 128), 0)
    head_lane = iota((kv_heads, 128), 1)
    new_k = jnp.zeros((kv_heads, 128), F32)
    new_v = jnp.zeros((kv_heads, 128), F32)
    for p in range(parts):
        piece = jnp.zeros((kv_heads, 128), F32)
        for h in range(kv_heads):
            piece = jnp.where(head_row == h, kvb[p * kv_heads + h], piece)
        here = (head_lane >> 5) == p
        new_k = jnp.where(here, pltpu.roll(piece, (32 * p - 64) % 128, 1), new_k)
        new_v = jnp.where(here, pltpu.roll(piece, (32 * p - 96) % 128, 1), new_v)
    ctab = jnp.broadcast_to(r["cs"][...], (kv_heads, 128))
    turned = pltpu.roll(ctab, 64, 1)
    front = head_lane < 64
    cosines = jnp.where(front, ctab, turned)
    sines = jnp.where(front, -turned, ctab)
    new_k = (new_k * cosines + pltpu.roll(new_k, 64, 1) * sines).astype(BF16).astype(F32)
    new_v = new_v.astype(BF16).astype(F32)
    new_score = jnp.zeros((8, 128), F32)
    for h in range(kv_heads):
        s = jnp.sum(qp[h, gy] * new_k[h:h + 1, :], axis=1, keepdims=True) * inv_root
        new_score = jnp.where(lane == h, s, new_score)
    o_recv()
    t = obuf[:, kv_heads].astype(F32)
    flat = t.reshape(ny * 8, 128)
    joined = flat + pltpu.roll(flat, 120, 1) + pltpu.roll(flat, 112, 1)
    valid = iota((ny * 8, 128), 1) < kv_heads
    peaks = jnp.where(valid, joined, 0.0).reshape(ny, 8, 128)
    masses = jnp.where(valid, pltpu.roll(joined, 104, 1), 0.0).reshape(ny, 8, 128)
    top = jnp.maximum(jnp.maximum(jnp.max(peaks, axis=0), own_peak), new_score)
    share = masses * jnp.exp(peaks - top[None])
    own_share = own_mass * jnp.exp(own_peak - top)
    new_share = jnp.exp(new_score - top)
    whole = jnp.sum(share, axis=0) + own_share + new_share
    inverse = 1.0 / jnp.where(lane < kv_heads, whole, 1.0)
    for h in range(kv_heads):
        got = jnp.sum(obuf[:, h].astype(F32) * share[:, :, h:h + 1], axis=0)
        got = got + own_out[h] * own_share[:, h:h + 1] + new_share[:, h:h + 1] * new_v[h:h + 1, :]
        att_out[h] = (got * inverse[:, h:h + 1]).astype(BF16)
    return [q_send, k_send, o_send]


def output_body(net, r, att_in, y_out):
    nx, ny, gx, gy = net.nx, net.ny, net.gx, net.gy
    agents, rows = nx * ny, ny
    ab, arow, ml = r["ab"], r["arow"], r["ml"]
    ab[gx] = att_in[gx]
    a_start, a_recv, a_send = net.exchange("gx", lambda p: att_in.at[p], ab, lambda i: i, r["ab_s"], r["ab_r"])
    a_start()
    ml[gx] = r["ml_in"][...]
    ml_start, ml_recv, ml_send = net.gather("gx", ml, r["ml_s"], r["ml_r"])
    ml_start()
    count = nx * 8
    target, source = iota((count, count), 0), iota((count, count), 1)
    turn = one_hot(source == lax.rem(target, nx) * 8 + target // nx)
    target, source = iota((agents, agents), 0), iota((agents, agents), 1)
    sort_rows = one_hot(source == lax.rem(target, ny) * nx + target // ny)
    adapters = index_columns(r["idx"])
    r["cols2"][...] = jnp.broadcast_to(adapters, (agents, 128))
    a_recv()
    turned = dot(turn, ab[...].astype(F32).reshape(count, 128).astype(BF16))
    for g in range(8):
        arow[gy, :, g * 128:(g + 1) * 128] = turned[g * nx:(g + 1) * nx, :].astype(BF16)
    g_start, g_recv, g_send = net.gather("gy", arow, r["ar_s"], r["ar_r"])
    g_start()
    width = nx * 128
    pattern_row, pattern_rank = iota((128, width), 0), iota((128, width), 1) & (RANK - 1)
    pattern = one_hot(((pattern_row & (RANK - 1)) == pattern_rank) & (pattern_row < 2 * RANK))
    g_recv()
    gathered = arow[...].astype(F32).reshape(agents, 1024).astype(BF16)
    attention = dot(sort_rows, gathered).astype(BF16)
    mixed = dot(attention, r["md"][...])
    lane = iota((agents, 128), 1)
    base = (gy * 2).astype(F32)
    first = (adapters == base) & (lane < RANK)
    second = (adapters == base + 1.0) & (lane >= RANK) & (lane < 2 * RANK)
    r["xl_src"][...] = jnp.where(first | second, mixed, 0.0).reshape(nx, rows, 128)
    r["xl"][gx] = r["xl_src"][gx]
    x_start, x_recv, x_send = net.scatter("gx", r["xl_src"], r["xl"], r["xl_s"], r["xl_r"])
    x_start()
    r["xm_src"][...] = dot(attention, r["wo"][...]).reshape(nx, rows, 256)
    r["xm"][gx] = r["xm_src"][gx]
    m_start, m_recv, m_send = net.scatter("gx", r["xm_src"], r["xm"], r["xm_s"], r["xm_r"])
    m_start()
    x_recv()
    zl = r["zl"]
    zl[gy] = jnp.sum(r["xl"][...], axis=0).astype(BF16)
    z_start, z_recv, z_send = net.gather("gy", zl, r["zl_s"], r["zl_r"])
    z_start()
    own_adapter = r["cols2"][pl.ds(pl.multiple_of(gx * rows, 8), rows), 0:1]
    m_recv()
    summed = jnp.sum(r["xm"][...], axis=0)
    ml_recv()
    lift_all = ml[...].reshape(width, 256)
    z_recv()
    lowmix = jnp.sum(zl[...].astype(F32), axis=0).astype(BF16)
    y = summed + ADAPTER_SCALE * dot(spread(lowmix, pattern, own_adapter), lift_all)
    ys, yb = r["ys"], r["yb"]
    for i in range(rows):
        ys[i] = y[i:i + 1, :]
    yb[gy] = ys[gy]
    y_start, y_recv, y_send = net.scatter("gy", ys, yb, r["y_s"], r["y_r"])
    y_start()
    y_recv()
    for i in range(ny):
        y_out[:, i * 256:(i + 1) * 256] = yb[i].astype(BF16)
    return [a_send, ml_send, g_send, x_send, m_send, z_send, y_send]


def vm(shape, dtype):
    return pltpu.VMEM(shape, dtype)


def pair(names, sizes):
    out = {}
    for name, n in zip(names, sizes):
        out[name + "_s"] = pltpu.SemaphoreType.DMA((n,))
        out[name + "_r"] = pltpu.SemaphoreType.DMA((n,))
    return out


def call(body, inputs, outs, scratch, net_args, axes, collective_id, in_specs=None):
    names_in, names_out, names_scratch = list(inputs), list(outs), list(scratch)

    def kernel(*refs):
        r = dict(zip(names_in + names_out + names_scratch, refs))
        net = Net(*net_args)
        net.barrier(axes)
        for wait in body(net, r):
            wait()

    specs = {n: pl.BlockSpec(memory_space=pltpu.VMEM) for n in names_in}
    specs.update(in_specs or {})
    return pl.pallas_call(
        kernel,
        out_shape=[outs[n] for n in names_out],
        in_specs=[specs[n] for n in names_in],
        out_specs=[pl.BlockSpec(memory_space=pltpu.VMEM)] * len(names_out),
        scratch_shapes=[scratch[n] for n in names_scratch],
        compiler_params=pltpu.CompilerParams(
            collective_id=collective_id, has_side_effects=True, vmem_limit_bytes=40 * 1024 * 1024),
    )(*[inputs[n] for n in names_in])


def make_local(nx, ny):
    agents, rows, width = nx * ny, ny, nx * 128

    def local(tokens, norm_gain, query_matrix, key_matrix, value_matrix, output_matrix, adapter_down,
              query_lift, key_value_lift, mixer_down, mixer_lift, adapter_index, suffix_lengths,
              shared_prefix_keys, shared_prefix_values, private_suffix_keys, private_suffix_values):
        zeros = lambda n, w: jnp.zeros((n, w), BF16)
        wcat = jnp.concatenate(
            [adapter_down[0], zeros(1024, 16), key_matrix, value_matrix, adapter_down[1], zeros(1024, 80)], axis=1)
        lift_in = jnp.concatenate(
            [query_lift.reshape(128, 256), zeros(128, 64),
             key_value_lift[:, 0].reshape(128, 32), key_value_lift[:, 1].reshape(128, 32)], axis=1)
        md = jnp.concatenate([mixer_down[0], mixer_down[1], zeros(1024, 96)], axis=1)
        position = (PREFIX_LENGTH + suffix_lengths).astype(F32)
        steps = jnp.arange(HEAD_SIZE // 2).astype(F32)
        frequency = jnp.power(F32(ROPE_BASE), -2.0 * steps / HEAD_SIZE)
        angles = position[:, None] * frequency[None, :]
        cs = jnp.concatenate([jnp.cos(angles), jnp.sin(angles)], axis=1)
        idx = adapter_index.reshape(1, agents)

        q, kv = call(
            lambda net, r: project_body(net, r, r["q"], r["kv"]),
            dict(tokens=tokens, gain=norm_gain.reshape(1, 1024), wq=query_matrix, wcat=wcat, lift_in=lift_in,
                 idx=idx, cs=cs),
            dict(q=jax.ShapeDtypeStruct((rows, 256), BF16), kv=jax.ShapeDtypeStruct((rows, 128), F32)),
            dict(tok=vm((ny, nx, 1152), BF16), lift=vm((nx, 128, 384), BF16), cols=vm((agents, 128), F32),
                 rl_src=vm((nx, rows, 128), F32), rl=vm((nx, rows, 128), F32),
                 rm_src=vm((nx, rows, 384), F32), rm=vm((nx, rows, 384), F32), al=vm((ny, rows, 128), BF16),
                 **pair(["tok", "lift", "rl", "rm", "al"], [ny, nx, nx, nx, ny])),
            (nx, ny), ("gy", "gx"), 0)
        (att,) = call(
            lambda net, r: attend_body(net, r, r["q"], r["kv"], r["att"]),
            dict(q=q, kv=kv, cs=cs, len=suffix_lengths, pk=shared_prefix_keys, pv=shared_prefix_values,
                 sk=private_suffix_keys, sv=private_suffix_values),
            dict(att=jax.ShapeDtypeStruct((nx, 8, 128), BF16)),
            dict(qbuf=vm((ny, rows, 256), BF16), kvs=vm((rows, 1, 128), F32), kvb=vm((rows, 1, 128), F32),
                 osend=vm((nx + 1, rows, 8, 128), BF16), obuf=vm((ny, nx + 1, 8, 128), BF16),
                 qp=vm((nx, rows, 8, 128), F32), **pair(["q", "kv", "o"], [ny, ny, ny])),
            (nx, ny), ("gy",), 1, dict(len=pl.BlockSpec(memory_space=pltpu.SMEM)))
        (y,) = call(
            lambda net, r: output_body(net, r, r["att"], r["y"]),
            dict(att=att, wo=output_matrix, md=md, ml_in=mixer_lift.reshape(128, 256), idx=idx),
            dict(y=jax.ShapeDtypeStruct((1, ny * 256), BF16)),
            dict(ab=vm((nx, 8, 128), BF16), arow=vm((ny, nx, 1024), BF16), ml=vm((nx, 128, 256), BF16),
                 cols2=vm((agents, 128), F32), xl_src=vm((nx, rows, 128), F32), xl=vm((nx, rows, 128), F32),
                 xm_src=vm((nx, rows, 256), F32), xm=vm((nx, rows, 256), F32), zl=vm((ny, rows, 128), BF16),
                 ys=vm((rows, 1, 256), F32), yb=vm((rows, 1, 256), F32),
                 **pair(["ab", "ml", "ar", "xl", "xm", "zl", "y"], [nx, nx, ny, nx, nx, ny, ny])),
            (nx, ny), ("gy", "gx"), 2)
        return y

    return local


def solution(mesh):
    return jax.shard_map(
        make_local(mesh.shape["gx"], mesh.shape["gy"]),
        mesh=mesh,
        in_specs=(
            P("gy", "gx"),
            P("gx"),
            P("gx", "gy"),
            P("gx", "gy"),
            P("gx", "gy"),
            P("gx", "gy"),
            P("gy", "gx", None),
            P("gx", None, "gy"),
            P("gx", None, None, "gy"),
            P("gy", "gx", None),
            P("gx", None, "gy"),
            P(),
            P(("gx", "gy")),
            P("gy", None),
            P("gy", None),
            P(("gx", "gy"), None, None),
            P(("gx", "gy"), None, None),
        ),
        out_specs=P(("gx", "gy"), None),
        check_vma=False,
    )
```

time: 748 us -> 151 us (0.20)
  blocking collectives: 565 us -> 0 us
  Pallas kernels: 0 us -> 134 us
  waiting for transfers between devices: 94.4 us -> 0 us
  local copies, waits for them, and re-layouts: 31.3 us -> 14.9 us
  between operations: 15.5 us -> 0.85 us
  other arithmetic: 14.6 us -> 0.38 us
  matrix products: 13 us -> 0 us
  starting transfers between devices: 9.51 us -> 0 us
    psum x2 -> x0, blocking collectives: 169 us -> none  [the longest x1 86.3 us: local(): adapter_update = lax.psum(down_part, ('gx', 'gy')).astype(jnp.bfloat16)]
    pallas_call x0 -> x3, Pallas kernels: none -> 134 us  [call(): pl.pallas_call(kernel, out_shape=[outs[n] for n in names_out], in_specs=[...]
    unnamed x2 -> x0, blocking collectives: 123 us -> none
    all_gather x3 -> x0, blocking collectives: 113 us -> none  [the longest x1 42.3 us: local(): gathered = lax.all_gather(tokens, 'gy', axis=0, tiled=True)]
    pmax x1 -> x0, blocking collectives: 113 us -> none  [local(): peak_all = lax.pmax(peak, 'gy')]
    unnamed x6 -> x0, waiting for transfers between devices: 85.7 us -> none
    all_to_all x2 -> x0, blocking collectives: 47.8 us -> none  [the longest x1 30.1 us: local(): lax.all_to_all(decode_attention, 'gx', split_axis=1, concat_axis=0, tiled...]
    unnamed x35 -> x31, local copies, waits for them, and re-layouts: 23.2 us -> 9.74 us
  transfers between devices with their start and end apart: 4 -> 0, of which waited for: 4 -> 0; matrix products, arithmetic and copies ran while one was open for 3% -> 0% of each run, Pallas kernels for 0% -> 0%
where the time goes in v1:
time: 151 us; the launch traced here: 150 us
  Pallas kernels  134 us (89%)
  local copies, waits for them, and re-layouts  14.9 us (10%)
    pallas_call x3, Pallas kernels, call(): pl.pallas_call(kernel, out_shape=[outs[n] for n in names_out], in_specs=[...  134 us
    unnamed x31, local copies, waits for them, and re-layouts  9.74 us

profile of v1, /device:TPU:1, one launch (start us, length us, event | category | flops | bytes accessed | tf_op | source)
XLA Modules:
  0.0 150.4 jit_solution(15389418257246148442)
XLA Ops:
  0.0 1.1 fusion.2
  1.2 0.8 copy.24
  2.0 1.0 copy.20
  3.0 1.7 %copy.21 = bf16[1024,32]{1,0:T(8,128)(2,1)} copy(bf16[1024,32]{0,1:T(8,128)(2,1)} %param.21) | data formatting | bytes 131072 | tf_op args[4]
  4.7 0.8 copy.25
  5.5 0.7 broadcast_in_dim.14
  6.3 0.8 broadcast_in_dim.15
  7.0 1.7 %concatenate.12.refs_3_ = bf16[1024,256]{1,0:T(8,128)(2,1)S(1)} concatenate(bf16[1024,48]{1,0:T(8,128)(2,1)} %bitcast.17, bf16[1024,16]{1,0:T(8,128)(2,1)} %broadcast_in_dim.14, bf16[1024,32]{1,0:T(8,128)(2,1)S(1)} %copy.20, bf16[1024,32]{1,0:T(8,128)(2,1)} %copy.21, bf16[1024,48]{1,0:T(8,128)(2,1)} %bitcast.18, bf16[1024,80]{1,0:T(8,128)(2,1)} %broadcast_in_dim.15), dimensions={1} | concatenate | bytes 1048576 | tf_op jit(solution)/shard_map/concatenate | solution.py:409
  8.7 0.8 fusion.4
  9.5 0.0 copy-done.10
  9.6 0.1 pad_maximum_fusion.refs_4_
  10.4 0.1 pad_maximum_fusion.1.refs_6_.refs_2_
  10.4 0.0 copy-done.9
  10.4 44.3 %shard_map.163 = (bf16[32,256]{1,0:T(8,128)(2,1)S(1)}, f32[32,128]{1,0:T(8,128)S(1)}) custom-call(bf16[8,1024]{1,0:T(8,128)(2,1)S(1)} %copy-done.7, f32[1,1024]{1,0:T(1,128)S(1)} %bitcast.12, bf16[1024,256]{1,0:T(8,128)(2,1)S(1)} %copy-done.4, bf16[1024,256]{1,0:T(8,128)(2,1)S(1)} %concatenate.12.refs_3_, bf16[128,384]{1,0:T(8,128)(2,1)S(1)} %pad_maximum_fusion.refs_4_, ...), custom_call_target="tpu_custom_call" | custom-call | tf_op jit(solution)/shard_map/pallas_call | solution.py:391
  54.8 0.0 copy-start
  54.8 2.2 %copy-done = bf16[1,2048,1024]{2,1,0:T(8,128)(2,1)S(1)} copy-done((bf16[1,2048,1024]{2,1,0:T(8,128)(2,1)S(1)}, bf16[1,2048,1024]{2,1,0:T(8,128)(2,1)}, u32[]{:S(2)}) %copy-start) | copy-done | bytes 4194328
  57.0 2.2 %copy-done.1 = bf16[1,2048,1024]{2,1,0:T(8,128)(2,1)S(1)} copy-done((bf16[1,2048,1024]{2,1,0:T(8,128)(2,1)S(1)}, bf16[1,2048,1024]{2,1,0:T(8,128)(2,1)}, u32[]{:S(2)}) %copy-start.1) | copy-done | bytes 4194328
  59.2 39.7 %shard_map.164.refs_0_ = bf16[8,8,128]{2,1,0:T(8,128)(2,1)S(1)} custom-call(bf16[32,256]{1,0:T(8,128)(2,1)S(1)} %get-tuple-element.7.refs_0_, f32[32,128]{1,0:T(8,128)S(1)} %get-tuple-element.8.refs_1_, f32[1,128]{1,0:T(1,128)S(1)} %pad_maximum_fusion.1.refs_6_.refs_2_, s32[1]{0:T(128)S(6)} %copy.29.refs_3_, bf16[512,1024]{1,0:T(8,128)(2,1)S(1)} %copy-done.2, ...), custom_call_target="tpu_custom_call" | custom-call | tf_op jit(solution)/shard_map/pallas_call | solution.py:391
  98.9 0.2 copy.27
  99.1 0.2 copy.26
  99.3 0.1 pad.2.clone
  99.4 0.2 maximum_maximum_fusion.refs_2_
  99.6 50.2 %shard_map.165 = bf16[1,8192]{1,0:T(2,128)(2,1)S(1)} custom-call(bf16[8,8,128]{2,1,0:T(8,128)(2,1)S(1)} %shard_map.164.refs_0_, bf16[1024,256]{1,0:T(8,128)(2,1)S(1)} %copy-done.5, bf16[1024,128]{1,0:T(8,128)(2,1)S(1)} %maximum_maximum_fusion.refs_2_, bf16[128,256]{1,0:T(8,128)(2,1)S(1)} %bitcast.11, s32[1,256]{1,0:T(1,128)S(1)} %bitcast.14), custom_call_target="tpu_custom_call" | custom-call | tf_op jit(solution)/shard_map/pallas_call | solution.py:391
  149.8 0.6 copy.30
  (24 shorter events, 0.1 us)
Async XLA Ops:
  0.0 10.4 %copy-start.7 = (bf16[8,1024]{1,0:T(8,128)(2,1)S(1)}, bf16[8,1024]{1,0:T(8,128)(2,1)}, u32[]{:S(2)}) copy-start(bf16[8,1024]{1,0:T(8,128)(2,1)} %refs_0_.1) | copy-start | bytes 49156
  0.0 10.4 %copy-start.8 = (f32[1024]{0:T(1024)S(1)}, f32[1024]{0:T(1024)}, u32[]{:S(2)}) copy-start(f32[1024]{0:T(1024)} %param.18) | copy-start | bytes 12292
  0.0 10.4 %copy-start.4 = (bf16[1024,256]{1,0:T(8,128)(2,1)S(1)}, bf16[1024,256]{1,0:T(8,128)(2,1)}, u32[]{:S(2)}) copy-start(bf16[1024,256]{1,0:T(8,128)(2,1)} %refs_2_.1) | copy-start | bytes 1572868
  0.0 9.5 %copy-start.10 = (bf16[8,16,256]{2,1,0:T(8,128)(2,1)S(1)}, bf16[8,16,256]{2,1,0:T(8,128)(2,1)}, u32[]{:S(2)}) copy-start(bf16[8,16,256]{2,1,0:T(8,128)(2,1)} %param.24) | copy-start | bytes 196612
  0.0 10.4 %copy-start.9 = (s32[256]{0:T(256)S(1)}, s32[256]{0:T(256)}, u32[]{:S(2)}) copy-start(s32[256]{0:T(256)} %param.28) | copy-start | bytes 3076
  0.0 54.7 %copy-start.2 = (bf16[512,1024]{1,0:T(8,128)(2,1)S(1)}, bf16[512,1024]{1,0:T(8,128)(2,1)}, u32[]{:S(2)}) copy-start(bf16[512,1024]{1,0:T(8,128)(2,1)} %refs_4_.1) | copy-start | bytes 3145732
  0.0 54.7 %copy-start.3 = (bf16[512,1024]{1,0:T(8,128)(2,1)S(1)}, bf16[512,1024]{1,0:T(8,128)(2,1)}, u32[]{:S(2)}) copy-start(bf16[512,1024]{1,0:T(8,128)(2,1)} %refs_5_.1) | copy-start | bytes 3145732
  54.8 2.2 %copy-start = (bf16[1,2048,1024]{2,1,0:T(8,128)(2,1)S(1)}, bf16[1,2048,1024]{2,1,0:T(8,128)(2,1)}, u32[]{:S(2)}) copy-start(bf16[1,2048,1024]{2,1,0:T(8,128)(2,1)} %refs_6_.1) | copy-start | bytes 12582916
  57.0 2.2 %copy-start.1 = (bf16[1,2048,1024]{2,1,0:T(8,128)(2,1)S(1)}, bf16[1,2048,1024]{2,1,0:T(8,128)(2,1)}, u32[]{:S(2)}) copy-start(bf16[1,2048,1024]{2,1,0:T(8,128)(2,1)} %refs_7_.1) | copy-start | bytes 12582916
  59.1 39.8 %copy-start.11 = (bf16[2,1024,16]{1,2,0:T(8,128)(2,1)S(1)}, bf16[2,1024,16]{1,2,0:T(8,128)(2,1)}, u32[]{:S(2)}) copy-start(bf16[2,1024,16]{1,2,0:T(8,128)(2,1)} %param.26) | copy-start | bytes 196612
  59.1 40.4 %copy-start.5 = (bf16[1024,256]{1,0:T(8,128)(2,1)S(1)}, bf16[1024,256]{1,0:T(8,128)(2,1)}, u32[]{:S(2)}) copy-start(bf16[1024,256]{1,0:T(8,128)(2,1)} %refs_1_.1) | copy-start | bytes 1572868
  59.1 40.4 %copy-start.6 = (bf16[8,16,256]{2,1,0:T(8,128)(2,1)S(1)}, bf16[8,16,256]{2,1,0:T(8,128)(2,1)}, u32[]{:S(2)}) copy-start(bf16[8,16,256]{2,1,0:T(8,128)(2,1)} %param.27) | copy-start | bytes 196612

commit v2 on v1

v2 whole, which is shorter than its diff:
```python
import math

import jax
import jax.numpy as jnp
from jax import lax
from jax.experimental import pallas as pl
from jax.experimental.pallas import tpu as pltpu
from jax.sharding import PartitionSpec as P

MODEL_WIDTH = 8192
HEAD_SIZE = 128
PREFIX_LENGTH = 16384
EPSILON = 1e-05
ADAPTER_SCALE = 2.0
ROPE_BASE = 500000.0
RANK = 16

MESH = pl.DeviceIdType.MESH
F32 = jnp.float32
BF16 = jnp.bfloat16
NEG = -1e30


def iota(shape, dim):
    return lax.broadcasted_iota(jnp.int32, shape, dim)


def one_hot(cond):
    return jnp.where(cond, 1.0, 0.0).astype(BF16)


def dot(a, b):
    return jnp.dot(a, b, preferred_element_type=F32)


def dot_t(a, b):
    return lax.dot_general(a, b, (((1,), (1,)), ((), ())), preferred_element_type=F32)


class Net:
    def __init__(self, gx_count, gy_count):
        self.nx, self.ny = gx_count, gy_count
        self.gx, self.gy = lax.axis_index("gx"), lax.axis_index("gy")
        self.nz = min(8, gy_count // 2)

    def along(self, axis):
        if axis == "gy":
            return self.gy, self.ny, lambda p: (self.gx, p)
        return self.gx, self.nx, lambda p: (p, self.gy)

    def signal_all(self):
        sem = pltpu.get_barrier_semaphore()
        for axis in ("gy", "gx"):
            me, n, dev = self.along(axis)

            def one(s, c):
                pl.semaphore_signal(sem, inc=1, device_id=dev(lax.rem(me + s, n)), device_id_type=MESH)
                return c

            lax.fori_loop(1, n, one, 0)

    def wait_all(self):
        pl.semaphore_wait(pltpu.get_barrier_semaphore(), self.nx + self.ny - 2)

    def exchange(self, axis, src_at, dst, slot, sems, all_src, all_dst):
        me, n, dev = self.along(axis)

        def start():
            def one(s, c):
                peer = lax.rem(me + s, n)
                pltpu.make_async_remote_copy(
                    src_ref=src_at(peer), dst_ref=dst.at[slot(me)], send_sem=sems.at[0], recv_sem=sems.at[1],
                    device_id=dev(peer), device_id_type=MESH).start()
                return c
            lax.fori_loop(1, n, one, 0)

        def whole():
            return pltpu.make_async_remote_copy(
                src_ref=all_src, dst_ref=all_dst, send_sem=sems.at[0], recv_sem=sems.at[1],
                device_id=dev(lax.rem(me + 1, n)), device_id_type=MESH)

        return start, lambda: whole().wait_recv(), lambda: whole().wait_send()

    def gather(self, axis, buf, sems):
        me, n, _ = self.along(axis)
        part = buf.at[pl.ds(0, n - 1)]
        return self.exchange(axis, lambda p: buf.at[me], buf, lambda i: i, sems, part, part)

    def scatter(self, axis, src, dst, sems):
        _, n, _ = self.along(axis)
        return self.exchange(axis, lambda p: src.at[p], dst, lambda i: i, sems,
                             src.at[pl.ds(0, n - 1)], dst.at[pl.ds(0, n - 1)])

    def relay(self, buf, sems, first_sems):
        nz = self.nz
        ny = self.ny // nz
        y, z = self.gy // nz, lax.rem(self.gy, nz)

        def copy(slot, recv, device):
            return pltpu.make_async_remote_copy(
                src_ref=buf.at[slot], dst_ref=buf.at[slot], send_sem=sems.at[0], recv_sem=recv,
                device_id=(self.gx, device), device_id_type=MESH)

        def send_on(slot):
            def one(t, c):
                copy(slot, sems.at[1], lax.rem(y + t, ny) * nz + z).start()
                return c
            lax.fori_loop(1, ny, one, 0)

        def start():
            def one(t, c):
                copy(self.gy, first_sems.at[z], y * nz + lax.rem(z + t, nz)).start()
                return c
            lax.fori_loop(1, nz, one, 0)
            send_on(self.gy)

        def wait_recv():
            def one(t, c):
                other = lax.rem(z + nz - t, nz)
                copy(y * nz + other, first_sems.at[other], y * nz + other).wait_recv()
                send_on(y * nz + other)
                return c
            lax.fori_loop(1, nz, one, 0)
            far = buf.at[pl.ds(0, (ny - 1) * nz)]
            pltpu.make_async_remote_copy(
                src_ref=far, dst_ref=far, send_sem=sems.at[0], recv_sem=sems.at[1],
                device_id=(self.gx, y * nz + lax.rem(z + 1, nz)), device_id_type=MESH).wait_recv()

        def wait_send():
            part = buf.at[pl.ds(0, self.ny - 1)]
            pltpu.make_async_remote_copy(
                src_ref=part, dst_ref=part, send_sem=sems.at[0], recv_sem=sems.at[1],
                device_id=(self.gx, y * nz + lax.rem(z + 1, nz)), device_id_type=MESH).wait_send()

        return start, wait_recv, wait_send


def index_columns(idx_ref):
    count = idx_ref.shape[1]
    row = jnp.broadcast_to(idx_ref[...].astype(F32), (count, count))
    diagonal = iota((count, count), 0) == iota((count, count), 1)
    return jnp.sum(jnp.where(diagonal, row, 0.0), axis=1, keepdims=True)


def spread(low, pattern, adapter_column):
    wide = dot(low, pattern)
    owner = (iota(wide.shape, 1) // RANK).astype(F32)
    return jnp.where(owner == adapter_column, wide, 0.0).astype(BF16)


def prepare(net, r, load):
    nx, ny, gx, gy = net.nx, net.ny, net.gx, net.gy
    agents = nx * ny
    tok, lift = r["tok"], r["lift"]
    lane = iota((8, 128), 1)
    frequency = jnp.exp((lane & 63).astype(F32) * (-2.0 * math.log(ROPE_BASE) / HEAD_SIZE))
    angles = (PREFIX_LENGTH + r["len"][0]).astype(F32) * frequency
    cs = jnp.where(lane < 64, jnp.cos(angles), jnp.sin(angles))
    r["cs"][...] = cs
    high = cs.astype(BF16).astype(F32)
    mid = (cs - high).astype(BF16).astype(F32)
    row = iota((8, 128), 0)
    parts = jnp.where(row == 0, high, jnp.where(row == 1, mid, jnp.where(row == 2, cs - high - mid, 0.0)))
    load("tokens")
    tok[gy, :, 0:1024] = r["tokens_v"][...]
    tok[gy, :, 1024:1152] = parts[0:nx].astype(BF16)
    ml = r["ml"]
    load("ml_in")
    ml[gx] = r["ml_in_v"][...]
    load("ql")
    load("kvl")
    place = iota((32, 128), 1) - iota((32, 128), 0)
    kvl = r["kvl_v"][...]
    lift[gx, :, 0:256] = r["ql_v"][...]
    lift[gx, :, 256:384] = (dot(kvl[:, 0].reshape(128, 32), one_hot(place == 64))
                            + dot(kvl[:, 1].reshape(128, 32), one_hot(place == 96))).astype(BF16)
    load("idx")
    r["cols"][...] = jnp.broadcast_to(index_columns(r["idx_v"]), (agents, 128))
    wc, md = r["wc"], r["md"]
    for name in ("down", "kt", "vt", "mdt"):
        load(name)
    wc[...] = jnp.zeros(wc.shape, BF16)
    wc[0:48] = r["down_v"][0]
    wc[128:176] = r["down_v"][1]
    wc[64:96] = r["kt_v"][...]
    wc[96:128] = r["vt_v"][...]
    md[...] = jnp.zeros(md.shape, BF16)
    md[0:16] = r["mdt_v"][0]
    md[16:32] = r["mdt_v"][1]


def project(net, r, load):
    nx, ny, gx, gy = net.nx, net.ny, net.gx, net.gy
    agents = nx * ny
    tok, lift = r["tok"], r["lift"]
    t_start, t_recv, t_send = net.relay(tok, r["tok_s"], r["tok_z"])
    l_start, l_recv, l_send = net.gather("gx", lift, r["lift_s"])
    t_start()
    l_start()
    load("gain")
    load("wq")
    t_recv()
    adapters = r["cols"][:, 0:1]
    x = tok[:, :, 0:1024].astype(F32).reshape(agents, 1024)
    scaled = (x * r["gain_v"][...]).astype(BF16)
    first = dot_t(scaled, r["wc"][...])
    squares = jnp.sum(x * x, axis=1, keepdims=True)
    lane = iota((agents, 128), 1)
    base = (gy * 2).astype(F32)
    down = jnp.where(adapters == base, first[:, 0:128],
                     jnp.where(adapters == base + 1.0, first[:, 128:256], 0.0))
    down = jnp.where(lane < 3 * RANK, down, jnp.where(lane == 127, squares, 0.0))
    rows = agents // nx
    r["rl_src"][...] = down.reshape(nx, rows, 128)
    rl_start, rl_recv, rl_send = net.scatter("gx", r["rl_src"], r["rl"], r["rl_s"])
    rl_start()
    r["rl"][gx] = r["rl_src"][gx]
    r["rm_src"][:, :, 256:384] = first[:, 0:128].reshape(nx, rows, 128)
    r["rm_src"][:, :, 0:256] = dot(scaled, r["wq_v"][...]).reshape(nx, rows, 256)
    rm_start, rm_recv, rm_send = net.scatter("gx", r["rm_src"], r["rm"], r["rm_s"])
    rm_start()
    r["rm"][gx] = r["rm_src"][gx]
    rl_recv()
    low = jnp.sum(r["rl"][...], axis=0)
    factor = lax.rsqrt(low[:, 127:128] / (nx * 1024) + EPSILON)
    al = r["al"]
    narrow = jnp.where(iota((rows, 128), 1) < 3 * RANK, low, 0.0)
    half = rows // 2
    al[gy] = (narrow[0:half] + pltpu.roll(narrow[half:rows], 64, 1)).astype(BF16)
    al_start, al_recv, al_send = net.gather("gy", al, r["al_s"])
    al_start()
    width = nx * 128
    pattern_row, pattern_rank = iota((128, width), 0), iota((128, width), 1) & (RANK - 1)
    patterns = [one_hot(pattern_row == pattern_rank + part * RANK) for part in range(3)]
    ctab = jnp.sum(tok[:, :, 1024:1152].astype(F32), axis=1)
    turned = pltpu.roll(ctab, 64, 1)
    front = iota(ctab.shape, 1) < 64
    cosines = jnp.where(front, ctab, turned)
    sines = jnp.where(front, -turned, ctab)
    own_adapter = r["cols"][pl.ds(pl.multiple_of(gx * rows, 8), rows), 0:1]
    rm_recv()
    summed = jnp.sum(r["rm"][...], axis=0)
    l_recv()
    ml_start, ml_recv, ml_send = net.gather("gx", r["ml"], r["ml_s"])
    ml_start()
    lift_all = lift[...].reshape(width, 384)
    al_recv()
    packed = jnp.sum(al[...].astype(F32), axis=0)
    lowrank = jnp.concatenate([packed, pltpu.roll(packed, 64, 1)], axis=0)
    lowrank = jnp.where(iota((rows, 128), 1) < 3 * RANK, lowrank, 0.0).astype(BF16)
    q_up = dot(spread(lowrank, patterns[0], own_adapter), lift_all[:, 0:256])
    k_up = dot(spread(lowrank, patterns[1], own_adapter), lift_all[:, 256:384])
    v_up = dot(spread(lowrank, patterns[2], own_adapter), lift_all[:, 256:384])
    q = (summed[:, 0:256] + ADAPTER_SCALE * q_up) * factor
    kv_up = jnp.where(iota((rows, 128), 1) < 96, k_up, v_up)
    kv = (summed[:, 256:384] + ADAPTER_SCALE * kv_up) * factor
    qbuf = r["qbuf"]
    for t in range(2):
        u = q[:, t * 128:(t + 1) * 128]
        qbuf[gy, :, t * 128:(t + 1) * 128] = (u * cosines + pltpu.roll(u, 64, 1) * sines).astype(BF16)
    return kv, ml_recv, [t_send, l_send, rl_send, rm_send, al_send, ml_send]


def attend(net, r, load, kv):
    nx, ny, gx, gy = net.nx, net.ny, net.gx, net.gy
    rows = ny
    kv_heads = nx
    parts = ny // kv_heads
    inv_root = 1.0 / math.sqrt(HEAD_SIZE)
    qbuf, kvs, kvb, osend, obuf, qp = r["qbuf"], r["kvs"], r["kvb"], r["osend"], r["obuf"], r["qp"]
    att_out = r["att"]
    q_start, q_recv, q_send = net.relay(qbuf, r["q_s"], r["q_z"])
    q_start()
    for i in range(rows):
        kvs[i] = kv[i:i + 1, :]

    def place(i):
        return lax.rem(i, parts) * kv_heads + i // parts

    kvb[place(gy)] = kvs[gy]
    k_start, k_recv, k_send = net.exchange("gy", lambda p: kvs.at[p], kvb, place, r["kv_s"],
                                           kvs.at[pl.ds(0, ny - 1)], kvb.at[pl.ds(0, ny - 1)])
    k_start()
    count = rows * 8
    target, source = iota((count, count), 0), iota((count, count), 1)
    perm = one_hot(source == (target & 7) * rows + (target >> 3))
    lane3 = iota((rows, 8, 128), 2)
    stats = jnp.zeros((rows, 8, 128), F32)
    for name in ("pk", "pv"):
        load(name)
    q_recv()
    for h in range(kv_heads):
        blocks = [qbuf[h * parts + j, :, t * 128:(t + 1) * 128] for j in range(parts) for t in range(2)]
        qh = dot(perm, jnp.concatenate(blocks, axis=0))
        qp[h] = qh.reshape(rows, 8, 128)
        scores = dot_t(qh.astype(BF16), r["pk_v"][:, h * 128:(h + 1) * 128]) * inv_root
        peak = jnp.max(scores, axis=1, keepdims=True)
        weights = jnp.exp(scores - peak)
        mass = jnp.sum(weights, axis=1, keepdims=True)
        out = dot(weights.astype(BF16), r["pv_v"][:, h * 128:(h + 1) * 128]) / mass
        osend[h] = out.reshape(rows, 8, 128).astype(BF16)
        here = (lane3 & 7) == h
        stats = jnp.where(here & (lane3 < 24), peak.reshape(rows, 8, 1), stats)
        stats = jnp.where(here & (lane3 >= 24) & (lane3 < 48), mass.reshape(rows, 8, 1), stats)
    high = stats.astype(BF16).astype(F32)
    mid = (stats - high).astype(BF16).astype(F32)
    low = stats - high - mid
    third = (lane3 >> 3)
    third = jnp.where(third >= 3, third - 3, third)
    coded = jnp.where(third == 0, high, jnp.where(third == 1, mid, low))
    osend[kv_heads] = jnp.where(lane3 < 48, coded, 0.0).astype(BF16)
    for h in range(kv_heads + 1):
        obuf[gy, h] = osend[h, gy]
    o_start, o_recv, o_send = net.exchange(
        "gy", lambda p: osend.at[:, p], obuf, lambda i: i, r["o_s"],
        osend.at[:, pl.ds(0, ny - 1)], obuf.at[pl.ds(0, ny - 1)])
    o_start()
    for name in ("sk", "sv"):
        load(name)
    span = r["sk_v"].shape[1]
    live = iota((8, span), 1) < r["len"][0]
    lane = iota((8, 128), 1)
    own_peak = jnp.zeros((8, 128), F32)
    own_mass = jnp.zeros((8, 128), F32)
    own_out = []
    for h in range(kv_heads):
        qh = qp[h, gy].astype(BF16)
        scores = dot_t(qh, r["sk_v"][0, :, h * 128:(h + 1) * 128]) * inv_root
        scores = jnp.where(live, scores, NEG)
        peak = jnp.max(scores, axis=1, keepdims=True)
        weights = jnp.exp(scores - peak)
        mass = jnp.sum(weights, axis=1, keepdims=True)
        own_out.append(dot(weights.astype(BF16), r["sv_v"][0, :, h * 128:(h + 1) * 128]) / mass)
        own_peak = jnp.where(lane == h, peak, own_peak)
        own_mass = jnp.where(lane == h, mass, own_mass)
    k_recv()
    head_row = iota((kv_heads, 128), 0)
    head_lane = iota((kv_heads, 128), 1)
    new_k = jnp.zeros((kv_heads, 128), F32)
    new_v = jnp.zeros((kv_heads, 128), F32)
    for p in range(parts):
        piece = jnp.zeros((kv_heads, 128), F32)
        for h in range(kv_heads):
            piece = jnp.where(head_row == h, kvb[p * kv_heads + h], piece)
        here = (head_lane >> 5) == p
        new_k = jnp.where(here, pltpu.roll(piece, (32 * p - 64) % 128, 1), new_k)
        new_v = jnp.where(here, pltpu.roll(piece, (32 * p - 96) % 128, 1), new_v)
    ctab = r["cs"][0:kv_heads]
    turned = pltpu.roll(ctab, 64, 1)
    front = head_lane < 64
    cosines = jnp.where(front, ctab, turned)
    sines = jnp.where(front, -turned, ctab)
    new_k = (new_k * cosines + pltpu.roll(new_k, 64, 1) * sines).astype(BF16).astype(F32)
    new_v = new_v.astype(BF16).astype(F32)
    new_score = jnp.zeros((8, 128), F32)
    for h in range(kv_heads):
        s = jnp.sum(qp[h, gy] * new_k[h:h + 1, :], axis=1, keepdims=True) * inv_root
        new_score = jnp.where(lane == h, s, new_score)
    o_recv()
    t = obuf[:, kv_heads].astype(F32)
    flat = t.reshape(ny * 8, 128)
    joined = flat + pltpu.roll(flat, 120, 1) + pltpu.roll(flat, 112, 1)
    valid = iota((ny * 8, 128), 1) < kv_heads
    peaks = jnp.where(valid, joined, 0.0).reshape(ny, 8, 128)
    masses = jnp.where(valid, pltpu.roll(joined, 104, 1), 0.0).reshape(ny, 8, 128)
    top = jnp.maximum(jnp.maximum(jnp.max(peaks, axis=0), own_peak), new_score)
    share = masses * jnp.exp(peaks - top[None])
    own_share = own_mass * jnp.exp(own_peak - top)
    new_share = jnp.exp(new_score - top)
    whole = jnp.sum(share, axis=0) + own_share + new_share
    inverse = 1.0 / jnp.where(lane < kv_heads, whole, 1.0)
    for h in range(kv_heads):
        got = jnp.sum(obuf[:, h].astype(F32) * share[:, :, h:h + 1], axis=0)
        got = got + own_out[h] * own_share[:, h:h + 1] + new_share[:, h:h + 1] * new_v[h:h + 1, :]
        att_out[h] = (got * inverse[:, h:h + 1]).astype(BF16)
    return [q_send, k_send, o_send]


def project_out(net, r, load, ml_recv, y_out):
    nx, ny, gx, gy = net.nx, net.ny, net.gx, net.gy
    agents, rows = nx * ny, ny
    ab, arow, ml = r["ab"], r["arow"], r["ml"]
    att_in = r["att"]
    ab[gx] = att_in[gx]
    a_start, a_recv, a_send = net.scatter("gx", att_in, ab, r["ab_s"])
    a_start()
    count = nx * 8
    target, source = iota((count, count), 0), iota((count, count), 1)
    turn = one_hot(source == lax.rem(target, nx) * 8 + target // nx)
    target, source = iota((agents, agents), 0), iota((agents, agents), 1)
    sort_rows = one_hot(source == lax.rem(target, ny) * nx + target // ny)
    adapters = r["cols"][:, 0:1]
    load("wo")
    a_recv()
    turned = dot(turn, ab[...].astype(F32).reshape(count, 128).astype(BF16))
    for g in range(8):
        arow[gy, :, g * 128:(g + 1) * 128] = turned[g * nx:(g + 1) * nx, :].astype(BF16)
    g_start, g_recv, g_send = net.relay(arow, r["ar_s"], r["ar_z"])
    g_start()
    width = nx * 128
    pattern_row, pattern_rank = iota((128, width), 0), iota((128, width), 1) & (RANK - 1)
    pattern = one_hot(((pattern_row & (RANK - 1)) == pattern_rank) & (pattern_row < 2 * RANK))
    g_recv()
    gathered = arow[...].astype(F32).reshape(agents, 1024).astype(BF16)
    attention = dot(sort_rows, gathered).astype(BF16)
    mixed = dot_t(attention, r["md"][...])
    lane = iota((agents, 128), 1)
    base = (gy * 2).astype(F32)
    first = (adapters == base) & (lane < RANK)
    second = (adapters == base + 1.0) & (lane >= RANK) & (lane < 2 * RANK)
    r["xl_src"][...] = jnp.where(first | second, mixed, 0.0).reshape(nx, rows, 128)
    r["xl"][gx] = r["xl_src"][gx]
    x_start, x_recv, x_send = net.scatter("gx", r["xl_src"], r["xl"], r["xl_s"])
    x_start()
    r["xm_src"][...] = dot(attention, r["wo_v"][...]).reshape(nx, rows, 256)
    r["xm"][gx] = r["xm_src"][gx]
    m_start, m_recv, m_send = net.scatter("gx", r["xm_src"], r["xm"], r["xm_s"])
    m_start()
    x_recv()
    zl = r["zl"]
    zl[gy] = jnp.sum(r["xl"][...], axis=0).astype(BF16)
    z_start, z_recv, z_send = net.gather("gy", zl, r["zl_s"])
    z_start()
    own_adapter = r["cols"][pl.ds(pl.multiple_of(gx * rows, 8), rows), 0:1]
    m_recv()
    summed = jnp.sum(r["xm"][...], axis=0)
    ml_recv()
    lift_all = ml[...].reshape(width, 256)
    z_recv()
    lowmix = jnp.sum(zl[...].astype(F32), axis=0).astype(BF16)
    y = summed + ADAPTER_SCALE * dot(spread(lowmix, pattern, own_adapter), lift_all)
    ys, yb = r["ys"], r["yb"]
    for i in range(rows):
        ys[i] = y[i:i + 1, :]
    yb[gy] = ys[gy]
    y_start, y_recv, y_send = net.scatter("gy", ys, yb, r["y_s"])
    y_start()
    y_recv()
    for i in range(ny):
        y_out[:, i * 256:(i + 1) * 256] = yb[i].astype(BF16)
    return [a_send, g_send, x_send, m_send, z_send, y_send]


def make_local(nx, ny):
    agents, rows = nx * ny, ny
    nz = min(8, ny // 2)
    sem = pltpu.SemaphoreType.DMA

    def local(tokens, norm_gain, query_matrix, key_matrix, value_matrix, output_matrix, adapter_down,
              query_lift, key_value_lift, mixer_down, mixer_lift, adapter_index, suffix_lengths,
              shared_prefix_keys, shared_prefix_values, private_suffix_keys, private_suffix_values):
        arrays = dict(
            tokens=tokens, ml_in=mixer_lift.reshape(128, 256), ql=query_lift.reshape(128, 256), kvl=key_value_lift,
            idx=adapter_index.reshape(1, agents), down=adapter_down.transpose(0, 2, 1), kt=key_matrix.T,
            vt=value_matrix.T, mdt=mixer_down.transpose(0, 2, 1), gain=norm_gain.reshape(1, 1024), wq=query_matrix,
            pk=shared_prefix_keys, pv=shared_prefix_values, sk=private_suffix_keys, sv=private_suffix_values,
            wo=output_matrix)
        scratch = {name + "_v": pltpu.VMEM(a.shape, a.dtype) for name, a in arrays.items()}
        scratch.update({name: pltpu.VMEM(shape, dtype) for name, shape, dtype in [
            ("tok", (ny, nx, 1152), BF16), ("lift", (nx, 128, 384), BF16), ("cols", (agents, 128), F32),
            ("cs", (8, 128), F32), ("wc", (256, 1024), BF16), ("md", (128, 1024), BF16),
            ("rl_src", (nx, rows, 128), F32), ("rl", (nx, rows, 128), F32),
            ("rm_src", (nx, rows, 384), F32), ("rm", (nx, rows, 384), F32), ("al", (ny, rows // 2, 128), BF16),
            ("qbuf", (ny, rows, 256), BF16), ("kvs", (rows, 1, 128), F32), ("kvb", (rows, 1, 128), F32),
            ("osend", (nx + 1, rows, 8, 128), BF16), ("obuf", (ny, nx + 1, 8, 128), BF16),
            ("qp", (nx, rows, 8, 128), F32), ("att", (nx, 8, 128), BF16),
            ("ab", (nx, 8, 128), BF16), ("arow", (ny, nx, 1024), BF16), ("ml", (nx, 128, 256), BF16),
            ("xl_src", (nx, rows, 128), F32), ("xl", (nx, rows, 128), F32),
            ("xm_src", (nx, rows, 256), F32), ("xm", (nx, rows, 256), F32), ("zl", (ny, rows, 128), BF16),
            ("ys", (rows, 1, 256), F32), ("yb", (rows, 1, 256), F32)]})
        phases = ["tok", "lift", "rl", "rm", "al", "q", "kv", "o", "ab", "ar", "ml", "xl", "xm", "zl", "y"]
        scratch.update({name + "_s": sem((2,)) for name in phases})
        scratch.update({name + "_z": sem((nz,)) for name in ("tok", "q", "ar")})
        scratch["loads"] = sem((len(arrays),))
        names, extra = list(arrays), list(scratch)

        def kernel(*refs):
            r = dict(zip(names + ["len", "y_out"] + extra, refs))
            copies = {name: pltpu.make_async_copy(r[name], r[name + "_v"], r["loads"].at[i])
                      for i, name in enumerate(names)}
            net = Net(nx, ny)
            net.signal_all()
            for name in names:
                copies[name].start()
            load = lambda name: copies[name].wait()
            prepare(net, r, load)
            net.wait_all()
            kv, ml_recv, waits = project(net, r, load)
            waits = waits + attend(net, r, load, kv)
            waits = waits + project_out(net, r, load, ml_recv, r["y_out"])
            for wait in waits:
                wait()

        any_space = pl.BlockSpec(memory_space=pl.ANY)
        return pl.pallas_call(
            kernel,
            out_shape=jax.ShapeDtypeStruct((1, ny * 256), BF16),
            in_specs=[any_space] * len(names) + [pl.BlockSpec(memory_space=pltpu.SMEM)],
            out_specs=pl.BlockSpec(memory_space=pltpu.VMEM),
            scratch_shapes=[scratch[n] for n in extra],
            compiler_params=pltpu.CompilerParams(
                collective_id=0, has_side_effects=True, vmem_limit_bytes=48 * 1024 * 1024),
        )(*arrays.values(), suffix_lengths)

    return local


def solution(mesh):
    return jax.shard_map(
        make_local(mesh.shape["gx"], mesh.shape["gy"]),
        mesh=mesh,
        in_specs=(
            P("gy", "gx"),
            P("gx"),
            P("gx", "gy"),
            P("gx", "gy"),
            P("gx", "gy"),
            P("gx", "gy"),
            P("gy", "gx", None),
            P("gx", None, "gy"),
            P("gx", None, None, "gy"),
            P("gy", "gx", None),
            P("gx", None, "gy"),
            P(),
            P(("gx", "gy")),
            P("gy", None),
            P("gy", None),
            P(("gx", "gy"), None, None),
            P(("gx", "gy"), None, None),
        ),
        out_specs=P(("gx", "gy"), None),
        check_vma=False,
    )
```

time: 151 us -> 116 us (0.77)
  Pallas kernels: 134 us -> 102 us
  local copies, waits for them, and re-layouts: 14.9 us -> 13.2 us
    pallas_call x3 -> x1, Pallas kernels: 134 us -> 102 us  [local(): pl.pallas_call(kernel, out_shape=jax.ShapeDtypeStruct((1, ny * 256), BF16...]
    unnamed x31 -> x29, local copies, waits for them, and re-layouts: 9.74 us -> 13.2 us
    slice x3 -> x0, local copies, waits for them, and re-layouts: 1.9 us -> none  [the longest x1 1.11 us: local(): adapter_down[1]]
    concatenate x3 -> x0, local copies, waits for them, and re-layouts: 1.78 us -> none  [the longest x1 1.7 us: local(): jnp.concatenate([adapter_down[0], zeros(1024, 16), key_matrix, value_matr...]
where the time goes in v2:
time: 116 us
  Pallas kernels  102 us (88%)
  local copies, waits for them, and re-layouts  13.2 us (11%)
    pallas_call x1, Pallas kernels, local(): pl.pallas_call(kernel, out_shape=jax.ShapeDtypeStruct((1, ny * 256), BF16...  102 us
    unnamed x29, local copies, waits for them, and re-layouts  13.2 us

profile of v2, /device:TPU:1, one launch (start us, length us, event | category | flops | bytes accessed | tf_op | source)
XLA Modules:
  0.0 115.8 jit_solution(14736901951023711950)
XLA Ops:
  0.7 0.0 copy-start
  0.7 1.2 %copy-done = bf16[512,1024]{1,0:T(8,128)(2,1)S(1)} copy-done((bf16[512,1024]{1,0:T(8,128)(2,1)S(1)}, bf16[512,1024]{1,0:T(8,128)(2,1)}, u32[]{:S(2)}) %copy-start) | copy-done | bytes 1048600
  1.9 0.0 copy-start.1
  1.9 1.2 %copy-done.1 = bf16[512,1024]{1,0:T(8,128)(2,1)S(1)} copy-done((bf16[512,1024]{1,0:T(8,128)(2,1)S(1)}, bf16[512,1024]{1,0:T(8,128)(2,1)}, u32[]{:S(2)}) %copy-start.1) | copy-done | bytes 1048600
  3.1 0.0 copy-start.2
  3.1 1.0 copy-done.2
  4.1 1.0 copy-done.3
  5.2 0.0 copy-start.4
  5.2 0.9 copy-done.4
  6.1 0.0 copy-start.5
  6.1 0.8 copy-done.5
  7.0 0.0 copy-start.6
  7.0 0.8 copy-done.6
  7.8 0.0 copy-start.7
  7.8 0.8 copy-done.7
  8.6 0.0 copy-start.8
  8.6 0.8 copy-done.8
  9.5 0.8 copy-done.9
  10.3 0.8 copy-done.10
  11.2 0.7 copy-done.11
  11.9 0.7 copy-done.12
  12.6 0.7 copy-done.13
  13.2 101.9 %shard_map.163 = bf16[1,8192]{1,0:T(2,128)(2,1)S(1)} custom-call(bf16[8,1024]{1,0:T(8,128)(2,1)S(1)} %copy-done.11, bf16[128,256]{1,0:T(8,128)(2,1)S(1)} %bitcast.9, bf16[128,256]{1,0:T(8,128)(2,1)S(1)} %bitcast.10, bf16[8,2,16,32]{3,2,1,0:T(8,128)(2,1)S(1)} %copy-done.7, s32[1,256]{1,0:T(1,128)S(1)} %bitcast.15, bf16[2,48,1024]{2,1,0:T(8,128)(2,1)S(1)} %bitcast.8, ...), custom_call_target="tpu_custom_call" | custom-call | tf_op jit(solution)/shard_map/pallas_call | solution.py:495
  115.2 0.6 copy.20
  (6 shorter events, 0.0 us)
Async XLA Ops:
  0.7 1.2 %copy-start = (bf16[512,1024]{1,0:T(8,128)(2,1)S(1)}, bf16[512,1024]{1,0:T(8,128)(2,1)}, u32[]{:S(2)}) copy-start(bf16[512,1024]{1,0:T(8,128)(2,1)} %refs_11_.1) | copy-start | bytes 3145732
  1.9 1.2 %copy-start.1 = (bf16[512,1024]{1,0:T(8,128)(2,1)S(1)}, bf16[512,1024]{1,0:T(8,128)(2,1)}, u32[]{:S(2)}) copy-start(bf16[512,1024]{1,0:T(8,128)(2,1)} %refs_12_.1) | copy-start | bytes 3145732
  3.1 1.0 copy-start.2
  4.1 1.0 copy-start.3
  5.2 0.9 copy-start.4
  6.1 0.8 copy-start.5
  7.0 0.8 copy-start.6
  7.8 0.8 copy-start.7
  8.6 0.8 copy-start.8
  9.5 0.8 copy-start.9
  10.3 0.8 copy-start.10
  11.2 0.7 copy-start.11
  11.9 0.7 copy-start.12
  12.6 0.7 copy-start.13

commit v3 on v2

--- a/solution.py
+++ b/solution.py
@@ -499,7 +499,7 @@
             out_specs=pl.BlockSpec(memory_space=pltpu.VMEM),
             scratch_shapes=[scratch[n] for n in extra],
             compiler_params=pltpu.CompilerParams(
-                collective_id=0, has_side_effects=True, vmem_limit_bytes=48 * 1024 * 1024),
+                collective_id=0, has_side_effects=True, vmem_limit_bytes=60 * 1024 * 1024),
         )(*arrays.values(), suffix_lengths)
 
     return local

time: 116 us -> 106 us (0.914)
  local copies, waits for them, and re-layouts: 13.2 us -> 1.41 us
    unnamed x29 -> x1, local copies, waits for them, and re-layouts: 13.2 us -> 1.41 us
    pallas_call x1, Pallas kernels: 102 us -> 103 us  [local(): pl.pallas_call(kernel, out_shape=jax.ShapeDtypeStruct((1, ny * 256), BF16...]
where the time goes in v3:
time: 106 us
  Pallas kernels  103 us (97%)
  local copies, waits for them, and re-layouts  1.41 us (1%)
    pallas_call x1, Pallas kernels, local(): pl.pallas_call(kernel, out_shape=jax.ShapeDtypeStruct((1, ny * 256), BF16...  103 us

profile of v3, /device:TPU:1, one launch (start us, length us, event | category | flops | bytes accessed | tf_op | source)
XLA Modules:
  0.0 105.5 jit_solution(9840128926760591333)
XLA Ops:
  0.7 103.5 %shard_map.163 = bf16[1,8192]{1,0:T(2,128)(2,1)} custom-call(bf16[8,1024]{1,0:T(8,128)(2,1)} %refs_0_.1, bf16[128,256]{1,0:T(8,128)(2,1)} %bitcast.9, bf16[128,256]{1,0:T(8,128)(2,1)} %bitcast.10, bf16[8,2,16,32]{3,2,1,0:T(8,128)(2,1)} %refs_3_.1, s32[1,256]{1,0:T(1,128)} %bitcast.15, bf16[2,48,1024]{2,1,0:T(8,128)(2,1)} %bitcast.8, ...), custom_call_target="tpu_custom_call" | custom-call | tf_op jit(solution)/shard_map/pallas_call | solution.py:495
  104.1 1.4 %copy.20 = bf16[1,8192]{1,0:T(2,128)(2,1)} copy(bf16[1,8192]{1,0:T(2,128)(2,1)} %shard_map.163) | data formatting | bytes 32768

commit v4 on v3

--- a/solution.py
+++ b/solution.py
@@ -42,6 +42,28 @@
         self.nx, self.ny = gx_count, gy_count
         self.gx, self.gy = lax.axis_index("gx"), lax.axis_index("gy")
         self.nz = min(8, gy_count // 2)
+        self.phases = []
+
+    def phase(self, start, wait_recv, wait_send):
+        done = dict(started=False, received=False)
+        self.phases.append((done, wait_recv, wait_send))
+
+        def begin():
+            done["started"] = True
+            start()
+
+        def receive():
+            done["received"] = True
+            wait_recv()
+
+        return begin, receive
+
+    def finish(self):
+        for done, wait_recv, wait_send in self.phases:
+            if done["started"]:
+                if not done["received"]:
+                    wait_recv()
+                wait_send()
 
     def along(self, axis):
         if axis == "gy":
@@ -62,14 +84,14 @@
     def wait_all(self):
         pl.semaphore_wait(pltpu.get_barrier_semaphore(), self.nx + self.ny - 2)
 
-    def exchange(self, axis, src_at, dst, slot, sems, all_src, all_dst):
+    def exchange(self, axis, src_at, dst_at, sems, all_src, all_dst):
         me, n, dev = self.along(axis)
 
         def start():
             def one(s, c):
                 peer = lax.rem(me + s, n)
                 pltpu.make_async_remote_copy(
-                    src_ref=src_at(peer), dst_ref=dst.at[slot(me)], send_sem=sems.at[0], recv_sem=sems.at[1],
+                    src_ref=src_at(peer), dst_ref=dst_at(me), send_sem=sems.at[0], recv_sem=sems.at[1],
                     device_id=dev(peer), device_id_type=MESH).start()
                 return c
             lax.fori_loop(1, n, one, 0)
@@ -79,19 +101,19 @@
                 src_ref=all_src, dst_ref=all_dst, send_sem=sems.at[0], recv_sem=sems.at[1],
                 device_id=dev(lax.rem(me + 1, n)), device_id_type=MESH)
 
-        return start, lambda: whole().wait_recv(), lambda: whole().wait_send()
+        return self.phase(start, lambda: whole().wait_recv(), lambda: whole().wait_send())
 
     def gather(self, axis, buf, sems):
         me, n, _ = self.along(axis)
         part = buf.at[pl.ds(0, n - 1)]
-        return self.exchange(axis, lambda p: buf.at[me], buf, lambda i: i, sems, part, part)
+        return self.exchange(axis, lambda p: buf.at[me], lambda i: buf.at[i], sems, part, part)
 
     def scatter(self, axis, src, dst, sems):
         _, n, _ = self.along(axis)
-        return self.exchange(axis, lambda p: src.at[p], dst, lambda i: i, sems,
+        return self.exchange(axis, lambda p: src.at[p], lambda i: dst.at[i], sems,
                              src.at[pl.ds(0, n - 1)], dst.at[pl.ds(0, n - 1)])
 
-    def relay(self, buf, sems, first_sems):
+    def relay(self, buf, sems, first_sems, far_sems):
         nz = self.nz
         ny = self.ny // nz
         y, z = self.gy // nz, lax.rem(self.gy, nz)
@@ -103,7 +125,7 @@
 
         def send_on(slot):
             def one(t, c):
-                copy(slot, sems.at[1], lax.rem(y + t, ny) * nz + z).start()
+                copy(slot, far_sems.at[y], lax.rem(y + t, ny) * nz + z).start()
                 return c
             lax.fori_loop(1, ny, one, 0)
 
@@ -114,25 +136,39 @@
             lax.fori_loop(1, nz, one, 0)
             send_on(self.gy)
 
-        def wait_recv():
+        def near():
             def one(t, c):
                 other = lax.rem(z + nz - t, nz)
                 copy(y * nz + other, first_sems.at[other], y * nz + other).wait_recv()
                 send_on(y * nz + other)
                 return c
             lax.fori_loop(1, nz, one, 0)
-            far = buf.at[pl.ds(0, (ny - 1) * nz)]
+
+        def far(other):
+            part = buf.at[pl.ds(other * nz, nz)]
             pltpu.make_async_remote_copy(
-                src_ref=far, dst_ref=far, send_sem=sems.at[0], recv_sem=sems.at[1],
-                device_id=(self.gx, y * nz + lax.rem(z + 1, nz)), device_id_type=MESH).wait_recv()
+                src_ref=part, dst_ref=part, send_sem=sems.at[0], recv_sem=far_sems.at[other],
+                device_id=(self.gx, other * nz + z), device_id_type=MESH).wait_recv()
+
+        def wait_recv():
+            near()
+            for t in range(1, ny):
+                far(lax.rem(y + t, ny))
 
         def wait_send():
             part = buf.at[pl.ds(0, self.ny - 1)]
             pltpu.make_async_remote_copy(
-                src_ref=part, dst_ref=part, send_sem=sems.at[0], recv_sem=sems.at[1],
+                src_ref=part, dst_ref=part, send_sem=sems.at[0], recv_sem=first_sems.at[0],
                 device_id=(self.gx, y * nz + lax.rem(z + 1, nz)), device_id_type=MESH).wait_send()
 
-        return start, wait_recv, wait_send
+        begin, receive = self.phase(start, wait_recv, wait_send)
+        done = self.phases[-1][0]
+
+        def near_then():
+            done["received"] = True
+            near()
+
+        return begin, receive, near_then, far
 
 
 def index_columns(idx_ref):
@@ -193,8 +229,8 @@
     nx, ny, gx, gy = net.nx, net.ny, net.gx, net.gy
     agents = nx * ny
     tok, lift = r["tok"], r["lift"]
-    t_start, t_recv, t_send = net.relay(tok, r["tok_s"], r["tok_z"])
-    l_start, l_recv, l_send = net.gather("gx", lift, r["lift_s"])
+    t_start, t_recv, _, _ = net.relay(tok, r["tok_s"], r["tok_z"], r["tok_f"])
+    l_start, l_recv = net.gather("gx", lift, r["lift_s"])
     t_start()
     l_start()
     load("gain")
@@ -209,29 +245,30 @@
     base = (gy * 2).astype(F32)
     down = jnp.where(adapters == base, first[:, 0:128],
                      jnp.where(adapters == base + 1.0, first[:, 128:256], 0.0))
-    down = jnp.where(lane < 3 * RANK, down, jnp.where(lane == 127, squares, 0.0))
+    down = jnp.where(lane < 3 * RANK, down, jnp.where(lane == 3 * RANK, squares, 0.0))
     rows = agents // nx
-    r["rl_src"][...] = down.reshape(nx, rows, 128)
-    rl_start, rl_recv, rl_send = net.scatter("gx", r["rl_src"], r["rl"], r["rl_s"])
+    half = rows // 2
+    down = down.reshape(nx, 2, half, 128)
+    r["rl_src"][...] = down[:, 0] + pltpu.roll(down[:, 1].reshape(nx * half, 128), 64, 1).reshape(nx, half, 128)
+    rl_start, rl_recv = net.scatter("gx", r["rl_src"], r["rl"], r["rl_s"])
     rl_start()
     r["rl"][gx] = r["rl_src"][gx]
     r["rm_src"][:, :, 256:384] = first[:, 0:128].reshape(nx, rows, 128)
     r["rm_src"][:, :, 0:256] = dot(scaled, r["wq_v"][...]).reshape(nx, rows, 256)
-    rm_start, rm_recv, rm_send = net.scatter("gx", r["rm_src"], r["rm"], r["rm_s"])
+    rm_start, rm_recv = net.scatter("gx", r["rm_src"], r["rm"], r["rm_s"])
     rm_start()
     r["rm"][gx] = r["rm_src"][gx]
     rl_recv()
     low = jnp.sum(r["rl"][...], axis=0)
-    factor = lax.rsqrt(low[:, 127:128] / (nx * 1024) + EPSILON)
     al = r["al"]
-    narrow = jnp.where(iota((rows, 128), 1) < 3 * RANK, low, 0.0)
-    half = rows // 2
-    al[gy] = (narrow[0:half] + pltpu.roll(narrow[half:rows], 64, 1)).astype(BF16)
-    al_start, al_recv, al_send = net.gather("gy", al, r["al_s"])
+    al[gy] = low.astype(BF16)
+    al_start, al_recv = net.gather("gy", al, r["al_s"])
     al_start()
     width = nx * 128
     pattern_row, pattern_rank = iota((128, width), 0), iota((128, width), 1) & (RANK - 1)
     patterns = [one_hot(pattern_row == pattern_rank + part * RANK) for part in range(3)]
+    square_columns = jnp.concatenate([low[:, 48:49], low[:, 112:113]], axis=0)
+    factor = lax.rsqrt(square_columns / (nx * 1024) + EPSILON)
     ctab = jnp.sum(tok[:, :, 1024:1152].astype(F32), axis=1)
     turned = pltpu.roll(ctab, 64, 1)
     front = iota(ctab.shape, 1) < 64
@@ -241,7 +278,7 @@
     rm_recv()
     summed = jnp.sum(r["rm"][...], axis=0)
     l_recv()
-    ml_start, ml_recv, ml_send = net.gather("gx", r["ml"], r["ml_s"])
+    ml_start, ml_recv = net.gather("gx", r["ml"], r["ml_s"])
     ml_start()
     lift_all = lift[...].reshape(width, 384)
     al_recv()
@@ -258,7 +295,25 @@
     for t in range(2):
         u = q[:, t * 128:(t + 1) * 128]
         qbuf[gy, :, t * 128:(t + 1) * 128] = (u * cosines + pltpu.roll(u, 64, 1) * sines).astype(BF16)
-    return kv, ml_recv, [t_send, l_send, rl_send, rm_send, al_send, ml_send]
+    return kv, ml_recv
+
+
+def coded_stats(peak, mass, lane, shift):
+    rows = peak.shape[0]
+    place = (lane - shift) & 127
+    value = jnp.where(place < 24, peak, mass)
+    high = value.astype(BF16).astype(F32)
+    mid = (value - high).astype(BF16).astype(F32)
+    low = value - high - mid
+    group = place >> 3
+    coded = jnp.where((group == 0) | (group == 3), high, jnp.where((group == 1) | (group == 4), mid, low))
+    mine = ((lane & 7) == (iota((rows, 128), 0) & 7)) & (group < 6)
+    return jnp.where(mine, coded, 0.0)
+
+
+def joined_stats(coded):
+    peaks = coded + pltpu.roll(coded, 120, 1) + pltpu.roll(coded, 112, 1)
+    return peaks, pltpu.roll(peaks, 104, 1)
 
 
 def attend(net, r, load, kv):
@@ -268,8 +323,7 @@
     parts = ny // kv_heads
     inv_root = 1.0 / math.sqrt(HEAD_SIZE)
     qbuf, kvs, kvb, osend, obuf, qp = r["qbuf"], r["kvs"], r["kvb"], r["osend"], r["obuf"], r["qp"]
-    att_out = r["att"]
-    q_start, q_recv, q_send = net.relay(qbuf, r["q_s"], r["q_z"])
+    q_start, _, q_near, q_far = net.relay(qbuf, r["q_s"], r["q_z"], r["q_f"])
     q_start()
     for i in range(rows):
         kvs[i] = kv[i:i + 1, :]
@@ -278,61 +332,55 @@
         return lax.rem(i, parts) * kv_heads + i // parts
 
     kvb[place(gy)] = kvs[gy]
-    k_start, k_recv, k_send = net.exchange("gy", lambda p: kvs.at[p], kvb, place, r["kv_s"],
-                                           kvs.at[pl.ds(0, ny - 1)], kvb.at[pl.ds(0, ny - 1)])
+    k_start, k_recv = net.exchange("gy", lambda p: kvs.at[p], lambda i: kvb.at[place(i)], r["kv_s"],
+                                   kvs.at[pl.ds(0, ny - 1)], kvb.at[pl.ds(0, ny - 1)])
     k_start()
     count = rows * 8
     target, source = iota((count, count), 0), iota((count, count), 1)
     perm = one_hot(source == (target & 7) * rows + (target >> 3))
-    lane3 = iota((rows, 8, 128), 2)
-    stats = jnp.zeros((rows, 8, 128), F32)
-    for name in ("pk", "pv"):
-        load(name)
-    q_recv()
-    for h in range(kv_heads):
+    lanes = iota((count, 128), 1)
+    shift = (gy & 15) * 8
+
+    def out_copy(head, agent, row, column):
+        return pltpu.make_async_remote_copy(
+            src_ref=osend.at[head, agent, pl.ds(0, 10)], dst_ref=obuf.at[row, column, pl.ds(0, 10)],
+            send_sem=r["o_s"].at[head], recv_sem=r["o_r"].at[row],
+            device_id=(head, agent), device_id_type=MESH)
+
+    def one_head(h):
+        columns = pl.ds(pl.multiple_of(h * 128, 128), 128)
         blocks = [qbuf[h * parts + j, :, t * 128:(t + 1) * 128] for j in range(parts) for t in range(2)]
         qh = dot(perm, jnp.concatenate(blocks, axis=0))
         qp[h] = qh.reshape(rows, 8, 128)
-        scores = dot_t(qh.astype(BF16), r["pk_v"][:, h * 128:(h + 1) * 128]) * inv_root
+        scores = dot_t(qh.astype(BF16), r["pk_v"][:, columns]) * inv_root
         peak = jnp.max(scores, axis=1, keepdims=True)
         weights = jnp.exp(scores - peak)
         mass = jnp.sum(weights, axis=1, keepdims=True)
-        out = dot(weights.astype(BF16), r["pv_v"][:, h * 128:(h + 1) * 128]) / mass
-        osend[h] = out.reshape(rows, 8, 128).astype(BF16)
-        here = (lane3 & 7) == h
-        stats = jnp.where(here & (lane3 < 24), peak.reshape(rows, 8, 1), stats)
-        stats = jnp.where(here & (lane3 >= 24) & (lane3 < 48), mass.reshape(rows, 8, 1), stats)
-    high = stats.astype(BF16).astype(F32)
-    mid = (stats - high).astype(BF16).astype(F32)
-    low = stats - high - mid
-    third = (lane3 >> 3)
-    third = jnp.where(third >= 3, third - 3, third)
-    coded = jnp.where(third == 0, high, jnp.where(third == 1, mid, low))
-    osend[kv_heads] = jnp.where(lane3 < 48, coded, 0.0).astype(BF16)
-    for h in range(kv_heads + 1):
-        obuf[gy, h] = osend[h, gy]
-    o_start, o_recv, o_send = net.exchange(
-        "gy", lambda p: osend.at[:, p], obuf, lambda i: i, r["o_s"],
-        osend.at[:, pl.ds(0, ny - 1)], obuf.at[pl.ds(0, ny - 1)])
-    o_start()
-    for name in ("sk", "sv"):
+        out = dot(weights.astype(BF16), r["pv_v"][:, columns]) / mass
+        osend[h, :, 0:8, :] = out.reshape(rows, 8, 128).astype(BF16)
+        coded = coded_stats(peak, mass, lanes, shift).reshape(rows, 8, 128)
+        line = jnp.sum(coded, axis=1, keepdims=True)
+        osend[h, :, 8:10, :] = jnp.broadcast_to(line, (rows, 2, 128)).astype(BF16)
+
+        def send(s, c):
+            out_copy(h, lax.rem(gy + s, ny), gx, gy).start()
+            return c
+
+        lax.fori_loop(jnp.where(h == gx, 1, 0), ny, send, 0)
+
+    for name in ("pk", "pv"):
         load(name)
-    span = r["sk_v"].shape[1]
-    live = iota((8, span), 1) < r["len"][0]
-    lane = iota((8, 128), 1)
-    own_peak = jnp.zeros((8, 128), F32)
-    own_mass = jnp.zeros((8, 128), F32)
-    own_out = []
-    for h in range(kv_heads):
-        qh = qp[h, gy].astype(BF16)
-        scores = dot_t(qh, r["sk_v"][0, :, h * 128:(h + 1) * 128]) * inv_root
-        scores = jnp.where(live, scores, NEG)
-        peak = jnp.max(scores, axis=1, keepdims=True)
-        weights = jnp.exp(scores - peak)
-        mass = jnp.sum(weights, axis=1, keepdims=True)
-        own_out.append(dot(weights.astype(BF16), r["sv_v"][0, :, h * 128:(h + 1) * 128]) / mass)
-        own_peak = jnp.where(lane == h, peak, own_peak)
-        own_mass = jnp.where(lane == h, mass, own_mass)
+    nz = net.nz
+    y_count, y = ny // nz, gy // nz
+    y_heads = nz // parts
+    q_near()
+    for t in [0] + sorted(range(1, y_count), key=lambda d: min(d, y_count - d)):
+        other = lax.rem(y + t, y_count)
+        if t:
+            q_far(other)
+        for i in range(y_heads):
+            one_head(other * y_heads + i)
+    obuf[gx, gy, 0:10, :] = osend[gx, gy, 0:10, :]
     k_recv()
     head_row = iota((kv_heads, 128), 0)
     head_lane = iota((kv_heads, 128), 1)
@@ -352,38 +400,110 @@
     sines = jnp.where(front, -turned, ctab)
     new_k = (new_k * cosines + pltpu.roll(new_k, 64, 1) * sines).astype(BF16).astype(F32)
     new_v = new_v.astype(BF16).astype(F32)
-    new_score = jnp.zeros((8, 128), F32)
+    for name in ("sk", "sv"):
+        load(name)
+    span = r["sk_v"].shape[1]
+    live = iota((8, span), 1) < r["len"][0]
+    lane = iota((8, 128), 1)
+    ss, sb = r["ss"], r["sb"]
     for h in range(kv_heads):
-        s = jnp.sum(qp[h, gy] * new_k[h:h + 1, :], axis=1, keepdims=True) * inv_root
-        new_score = jnp.where(lane == h, s, new_score)
+        q_own = qp[h, gy]
+        scores = dot_t(q_own.astype(BF16), r["sk_v"][0, :, h * 128:(h + 1) * 128]) * inv_root
+        scores = jnp.where(live, scores, NEG)
+        new_score = jnp.sum(q_own * new_k[h:h + 1, :], axis=1, keepdims=True) * inv_root
+        peak = jnp.maximum(jnp.max(scores, axis=1, keepdims=True), new_score)
+        weights = jnp.exp(scores - peak)
+        new_weight = jnp.exp(new_score - peak)
+        mass = jnp.sum(weights, axis=1, keepdims=True) + new_weight
+        mixed = dot(weights.astype(BF16), r["sv_v"][0, :, h * 128:(h + 1) * 128]) + new_weight * new_v[h:h + 1, :]
+        ss[h, 0:8, :] = (mixed / mass).astype(BF16)
+        line = jnp.sum(coded_stats(peak, mass, lane, 0), axis=0, keepdims=True)
+        ss[h, 8:10, :] = jnp.broadcast_to(line, (2, 128)).astype(BF16)
+    sb[gx, 0:10, :] = ss[gx, 0:10, :]
+    s_start, s_recv = net.exchange(
+        "gx", lambda p: ss.at[p, pl.ds(0, 10)], lambda i: sb.at[i, pl.ds(0, 10)], r["ss_s"],
+        ss.at[pl.ds(0, nx - 1), pl.ds(0, 10)], sb.at[pl.ds(0, nx - 1), pl.ds(0, 10)])
+    s_start()
+
+    def out_all(ref, t, own_row):
+        row = lax.rem(gx + t, nx)
+        span_rows = ref.at[row, pl.ds(0, ny - 1 if t == 0 else ny), pl.ds(0, 10)]
+        return pltpu.make_async_remote_copy(
+            src_ref=span_rows, dst_ref=span_rows, send_sem=r["o_s"].at[row], recv_sem=r["o_r"].at[row],
+            device_id=(gx, lax.rem(gy + 1, ny)), device_id_type=MESH)
+
+    def o_recv():
+        for t in range(nx):
+            out_all(obuf, t, 0).wait_recv()
+
+    def o_send():
+        for t in range(nx):
+            out_all(osend, t, 0).wait_send()
+
+    o_start, o_recv = net.phase(lambda: None, o_recv, o_send)
+    o_start()
+    s_recv()
     o_recv()
-    t = obuf[:, kv_heads].astype(F32)
-    flat = t.reshape(ny * 8, 128)
-    joined = flat + pltpu.roll(flat, 120, 1) + pltpu.roll(flat, 112, 1)
-    valid = iota((ny * 8, 128), 1) < kv_heads
-    peaks = jnp.where(valid, joined, 0.0).reshape(ny, 8, 128)
-    masses = jnp.where(valid, pltpu.roll(joined, 104, 1), 0.0).reshape(ny, 8, 128)
-    top = jnp.maximum(jnp.maximum(jnp.max(peaks, axis=0), own_peak), new_score)
-    share = masses * jnp.exp(peaks - top[None])
+    sub = iota((8, 128), 0)
+    line_row, line_lane = iota((ny, 128), 0), iota((ny, 128), 1)
+    here = (line_lane >> 3) == (line_row & 15)
+    zero = jnp.zeros((nx, 128), F32)
+    halves = max(1, ny // 16)
+    size = ny // halves
+    agent_row = iota((nx, 128), 0)
+    peaks, masses = [jnp.full((nx, 128), NEG, F32)] * halves, [zero] * halves
+    own = zero
+    for i in range(nx):
+        coded = obuf[i, :, 8:10, :].astype(F32)[:, 0, :]
+        peak, mass = joined_stats(coded)
+        peak, mass = jnp.where(here, peak, 0.0), jnp.where(here, mass, 0.0)
+        for k in range(halves):
+            part = slice(k * size, (k + 1) * size)
+            peaks[k] = jnp.where(agent_row == i, jnp.sum(peak[part], axis=0, keepdims=True), peaks[k])
+            masses[k] = jnp.where(agent_row == i, jnp.sum(mass[part], axis=0, keepdims=True), masses[k])
+        own = jnp.where(agent_row == i, sb[i, 8:10, :].astype(F32)[0:1, :], own)
+    if size < 16:
+        there = iota((nx, 128), 1) < size * 8
+        peaks = [jnp.where(there, p, NEG) for p in peaks]
+    own_peak, own_mass = joined_stats(own)
+    first = iota((nx, 128), 1) < 8
+    own_peak, own_mass = jnp.where(first, own_peak, 0.0), jnp.where(first, own_mass, 0.0)
+    for step in (8, 16, 32, 64):
+        own_peak = own_peak + pltpu.roll(own_peak, step, 1)
+        own_mass = own_mass + pltpu.roll(own_mass, step, 1)
+    top = peaks[0]
+    for p in peaks[1:]:
+        top = jnp.maximum(top, p)
+    for step in (8, 16, 32, 64):
+        top = jnp.maximum(top, pltpu.roll(top, step, 1))
+    top = jnp.maximum(top, own_peak)
+    shares = [m * jnp.exp(p - top) for m, p in zip(masses, peaks)]
     own_share = own_mass * jnp.exp(own_peak - top)
-    new_share = jnp.exp(new_score - top)
-    whole = jnp.sum(share, axis=0) + own_share + new_share
-    inverse = 1.0 / jnp.where(lane < kv_heads, whole, 1.0)
-    for h in range(kv_heads):
-        got = jnp.sum(obuf[:, h].astype(F32) * share[:, :, h:h + 1], axis=0)
-        got = got + own_out[h] * own_share[:, h:h + 1] + new_share[:, h:h + 1] * new_v[h:h + 1, :]
-        att_out[h] = (got * inverse[:, h:h + 1]).astype(BF16)
-    return [q_send, k_send, o_send]
+    whole = shares[0]
+    for share in shares[1:]:
+        whole = whole + share
+    for step in (8, 16, 32, 64):
+        whole = whole + pltpu.roll(whole, step, 1)
+    inverse = 1.0 / (whole + own_share)
+    diagonal = (lane & 7) == sub
+    att = r["att"]
+    for i in range(nx):
+        wide = jnp.concatenate(
+            [jnp.where(diagonal, share[i:i + 1, :] * inverse[i:i + 1, :], 0.0) for share in shares], axis=1)
+        wide = wide[:, 0:ny * 8]
+        high = wide.astype(BF16)
+        both = jnp.concatenate([high.astype(F32), wide - high.astype(F32)], axis=0).astype(BF16)
+        values = obuf[i, :, 0:8, :].astype(F32).reshape(ny * 8, 128).astype(BF16)
+        mixed = dot(both, values)
+        column = jnp.sum(jnp.where(lane == sub, own_share[i:i + 1, :] * inverse[i:i + 1, :], 0.0),
+                         axis=1, keepdims=True)
+        att[i] = mixed[0:8] + mixed[8:16] + column * sb[i, 0:8, :].astype(F32)
 
 
 def project_out(net, r, load, ml_recv, y_out):
     nx, ny, gx, gy = net.nx, net.ny, net.gx, net.gy
     agents, rows = nx * ny, ny
-    ab, arow, ml = r["ab"], r["arow"], r["ml"]
-    att_in = r["att"]
-    ab[gx] = att_in[gx]
-    a_start, a_recv, a_send = net.scatter("gx", att_in, ab, r["ab_s"])
-    a_start()
+    arow, ml = r["arow"], r["ml"]
     count = nx * 8
     target, source = iota((count, count), 0), iota((count, count), 1)
     turn = one_hot(source == lax.rem(target, nx) * 8 + target // nx)
@@ -391,11 +511,10 @@
     sort_rows = one_hot(source == lax.rem(target, ny) * nx + target // ny)
     adapters = r["cols"][:, 0:1]
     load("wo")
-    a_recv()
-    turned = dot(turn, ab[...].astype(F32).reshape(count, 128).astype(BF16))
+    turned = dot(turn, r["att"][...].reshape(count, 128).astype(BF16))
     for g in range(8):
         arow[gy, :, g * 128:(g + 1) * 128] = turned[g * nx:(g + 1) * nx, :].astype(BF16)
-    g_start, g_recv, g_send = net.relay(arow, r["ar_s"], r["ar_z"])
+    g_start, g_recv, _, _ = net.relay(arow, r["ar_s"], r["ar_z"], r["ar_f"])
     g_start()
     width = nx * 128
     pattern_row, pattern_rank = iota((128, width), 0), iota((128, width), 1) & (RANK - 1)
@@ -408,18 +527,24 @@
     base = (gy * 2).astype(F32)
     first = (adapters == base) & (lane < RANK)
     second = (adapters == base + 1.0) & (lane >= RANK) & (lane < 2 * RANK)
-    r["xl_src"][...] = jnp.where(first | second, mixed, 0.0).reshape(nx, rows, 128)
+    quarter = rows // 4
+    mixed = jnp.where(first | second, mixed, 0.0).reshape(nx, 4, quarter, 128)
+    packed = mixed[:, 0]
+    for k in range(1, 4):
+        turned = pltpu.roll(mixed[:, k].reshape(nx * quarter, 128), 32 * k, 1)
+        packed = packed + turned.reshape(nx, quarter, 128)
+    r["xl_src"][...] = packed
     r["xl"][gx] = r["xl_src"][gx]
-    x_start, x_recv, x_send = net.scatter("gx", r["xl_src"], r["xl"], r["xl_s"])
+    x_start, x_recv = net.scatter("gx", r["xl_src"], r["xl"], r["xl_s"])
     x_start()
     r["xm_src"][...] = dot(attention, r["wo_v"][...]).reshape(nx, rows, 256)
     r["xm"][gx] = r["xm_src"][gx]
-    m_start, m_recv, m_send = net.scatter("gx", r["xm_src"], r["xm"], r["xm_s"])
+    m_start, m_recv = net.scatter("gx", r["xm_src"], r["xm"], r["xm_s"])
     m_start()
     x_recv()
     zl = r["zl"]
     zl[gy] = jnp.sum(r["xl"][...], axis=0).astype(BF16)
-    z_start, z_recv, z_send = net.gather("gy", zl, r["zl_s"])
+    z_start, z_recv = net.gather("gy", zl, r["zl_s"])
     z_start()
     own_adapter = r["cols"][pl.ds(pl.multiple_of(gx * rows, 8), rows), 0:1]
     m_recv()
@@ -427,18 +552,19 @@
     ml_recv()
     lift_all = ml[...].reshape(width, 256)
     z_recv()
-    lowmix = jnp.sum(zl[...].astype(F32), axis=0).astype(BF16)
+    packed = jnp.sum(zl[...].astype(F32), axis=0)
+    lowmix = jnp.concatenate([packed] + [pltpu.roll(packed, 128 - 32 * k, 1) for k in range(1, 4)], axis=0)
+    lowmix = jnp.where(iota((rows, 128), 1) < 2 * RANK, lowmix, 0.0).astype(BF16)
     y = summed + ADAPTER_SCALE * dot(spread(lowmix, pattern, own_adapter), lift_all)
     ys, yb = r["ys"], r["yb"]
     for i in range(rows):
         ys[i] = y[i:i + 1, :]
     yb[gy] = ys[gy]
-    y_start, y_recv, y_send = net.scatter("gy", ys, yb, r["y_s"])
+    y_start, y_recv = net.scatter("gy", ys, yb, r["y_s"])
     y_start()
     y_recv()
     for i in range(ny):
         y_out[:, i * 256:(i + 1) * 256] = yb[i].astype(BF16)
-    return [a_send, g_send, x_send, m_send, z_send, y_send]
 
 
 def make_local(nx, ny):
@@ -459,18 +585,21 @@
         scratch.update({name: pltpu.VMEM(shape, dtype) for name, shape, dtype in [
             ("tok", (ny, nx, 1152), BF16), ("lift", (nx, 128, 384), BF16), ("cols", (agents, 128), F32),
             ("cs", (8, 128), F32), ("wc", (256, 1024), BF16), ("md", (128, 1024), BF16),
-            ("rl_src", (nx, rows, 128), F32), ("rl", (nx, rows, 128), F32),
+            ("rl_src", (nx, rows // 2, 128), F32), ("rl", (nx, rows // 2, 128), F32),
             ("rm_src", (nx, rows, 384), F32), ("rm", (nx, rows, 384), F32), ("al", (ny, rows // 2, 128), BF16),
             ("qbuf", (ny, rows, 256), BF16), ("kvs", (rows, 1, 128), F32), ("kvb", (rows, 1, 128), F32),
-            ("osend", (nx + 1, rows, 8, 128), BF16), ("obuf", (ny, nx + 1, 8, 128), BF16),
-            ("qp", (nx, rows, 8, 128), F32), ("att", (nx, 8, 128), BF16),
-            ("ab", (nx, 8, 128), BF16), ("arow", (ny, nx, 1024), BF16), ("ml", (nx, 128, 256), BF16),
-            ("xl_src", (nx, rows, 128), F32), ("xl", (nx, rows, 128), F32),
-            ("xm_src", (nx, rows, 256), F32), ("xm", (nx, rows, 256), F32), ("zl", (ny, rows, 128), BF16),
+            ("osend", (nx, rows, 16, 128), BF16), ("obuf", (nx, ny, 16, 128), BF16),
+            ("ss", (nx, 16, 128), BF16), ("sb", (nx, 16, 128), BF16),
+            ("qp", (nx, rows, 8, 128), F32), ("att", (nx, 8, 128), F32),
+            ("arow", (ny, nx, 1024), BF16), ("ml", (nx, 128, 256), BF16),
+            ("xl_src", (nx, rows // 4, 128), F32), ("xl", (nx, rows // 4, 128), F32),
+            ("xm_src", (nx, rows, 256), F32), ("xm", (nx, rows, 256), F32), ("zl", (ny, rows // 4, 128), BF16),
             ("ys", (rows, 1, 256), F32), ("yb", (rows, 1, 256), F32)]})
-        phases = ["tok", "lift", "rl", "rm", "al", "q", "kv", "o", "ab", "ar", "ml", "xl", "xm", "zl", "y"]
+        phases = ["tok", "lift", "rl", "rm", "al", "q", "kv", "ss", "ar", "ml", "xl", "xm", "zl", "y"]
         scratch.update({name + "_s": sem((2,)) for name in phases})
         scratch.update({name + "_z": sem((nz,)) for name in ("tok", "q", "ar")})
+        scratch.update({name + "_f": sem((ny // nz,)) for name in ("tok", "q", "ar")})
+        scratch.update(o_s=sem((nx,)), o_r=sem((nx,)))
         scratch["loads"] = sem((len(arrays),))
         names, extra = list(arrays), list(scratch)
 
@@ -485,11 +614,10 @@
             load = lambda name: copies[name].wait()
             prepare(net, r, load)
             net.wait_all()
-            kv, ml_recv, waits = project(net, r, load)
-            waits = waits + attend(net, r, load, kv)
-            waits = waits + project_out(net, r, load, ml_recv, r["y_out"])
-            for wait in waits:
-                wait()
+            kv, ml_recv = project(net, r, load)
+            attend(net, r, load, kv)
+            project_out(net, r, load, ml_recv, r["y_out"])
+            net.finish()
 
         any_space = pl.BlockSpec(memory_space=pl.ANY)
         return pl.pallas_call(

time: 106 us -> 98.9 us (0.933)
  Pallas kernels: 103 us -> 96.7 us
    pallas_call x1, Pallas kernels: 103 us -> 96.7 us  [local(): pl.pallas_call(kernel, out_shape=jax.ShapeDtypeStruct((1, ny * 256), BF16...]
where the time goes in v4:
time: 98.9 us; the launch traced here: 98.7 us
  Pallas kernels  96.7 us (98%)
  local copies, waits for them, and re-layouts  1.41 us (1%)
    pallas_call x1, Pallas kernels, local(): pl.pallas_call(kernel, out_shape=jax.ShapeDtypeStruct((1, ny * 256), BF16...  96.7 us

profile of v4, /device:TPU:1, one launch (start us, length us, event | category | flops | bytes accessed | tf_op | source)
XLA Modules:
  0.0 98.7 jit_solution(17694487079147322521)
XLA Ops:
  0.7 96.7 %shard_map.163 = bf16[1,8192]{1,0:T(2,128)(2,1)} custom-call(bf16[8,1024]{1,0:T(8,128)(2,1)} %refs_0_.1, bf16[128,256]{1,0:T(8,128)(2,1)} %bitcast.9, bf16[128,256]{1,0:T(8,128)(2,1)} %bitcast.10, bf16[8,2,16,32]{3,2,1,0:T(8,128)(2,1)} %refs_3_.1, s32[1,256]{1,0:T(1,128)} %bitcast.15, bf16[2,48,1024]{2,1,0:T(8,128)(2,1)} %bitcast.8, ...), custom_call_target="tpu_custom_call" | custom-call | tf_op jit(solution)/shard_map/pallas_call | solution.py:623
  97.3 1.4 %copy.20 = bf16[1,8192]{1,0:T(2,128)(2,1)} copy(bf16[1,8192]{1,0:T(2,128)(2,1)} %shard_map.163) | data formatting | bytes 32768

commit v5 on v4

--- a/solution.py
+++ b/solution.py
@@ -42,6 +42,7 @@
         self.nx, self.ny = gx_count, gy_count
         self.gx, self.gy = lax.axis_index("gx"), lax.axis_index("gy")
         self.nz = min(8, gy_count // 2)
+        self.y, self.z = self.gy // self.nz, lax.rem(self.gy, self.nz)
         self.phases = []
 
     def phase(self, start, wait_recv, wait_send):
@@ -68,6 +69,10 @@
     def along(self, axis):
         if axis == "gy":
             return self.gy, self.ny, lambda p: (self.gx, p)
+        if axis == "z":
+            return self.z, self.nz, lambda p: (self.gx, self.y * self.nz + p)
+        if axis == "y":
+            return self.y, self.ny // self.nz, lambda p: (self.gx, p * self.nz + self.z)
         return self.gx, self.nx, lambda p: (p, self.gy)
 
     def signal_all(self):
@@ -225,6 +230,15 @@
     md[16:32] = r["mdt_v"][1]
 
 
+def swap_blocks(net, r, name):
+    source, target = r[name + "_v"], r[name + "_all"]
+    width = target.shape[2]
+    count = target.shape[0]
+    columns = lambda i: pl.ds(pl.multiple_of(i * width, 128), width)
+    part = target.at[pl.ds(0, count - 1)]
+    return net.exchange("y", lambda p: source.at[:, columns(p)], lambda i: target.at[i], r[name + "_s"], part, part)
+
+
 def project(net, r, load):
     nx, ny, gx, gy = net.nx, net.ny, net.gx, net.gy
     agents = nx * ny
@@ -235,7 +249,12 @@
     l_start()
     load("gain")
     load("wq")
+    for name in ("pk", "pv"):
+        load(name)
     t_recv()
+    swaps = [swap_blocks(net, r, name) for name in ("pk", "pv")]
+    for swap_start, _ in swaps:
+        swap_start()
     adapters = r["cols"][:, 0:1]
     x = tok[:, :, 0:1024].astype(F32).reshape(agents, 1024)
     scaled = (x * r["gain_v"][...]).astype(BF16)
@@ -292,10 +311,12 @@
     kv_up = jnp.where(iota((rows, 128), 1) < 96, k_up, v_up)
     kv = (summed[:, 256:384] + ADAPTER_SCALE * kv_up) * factor
     qbuf = r["qbuf"]
+    heads = []
     for t in range(2):
         u = q[:, t * 128:(t + 1) * 128]
-        qbuf[gy, :, t * 128:(t + 1) * 128] = (u * cosines + pltpu.roll(u, 64, 1) * sines).astype(BF16)
-    return kv, ml_recv
+        heads.append((u * cosines + pltpu.roll(u, 64, 1) * sines).astype(BF16))
+        qbuf[net.z, :, t * 128:(t + 1) * 128] = heads[t]
+    return jnp.concatenate([h.astype(F32) for h in heads] + [kv], axis=1), ml_recv, swaps
 
 
 def coded_stats(peak, mass, lane, shift):
@@ -316,17 +337,19 @@
     return peaks, pltpu.roll(peaks, 104, 1)
 
 
-def attend(net, r, load, kv):
+def attend(net, r, load, qkv, swaps):
     nx, ny, gx, gy = net.nx, net.ny, net.gx, net.gy
+    nz, y, z = net.nz, net.y, net.z
     rows = ny
     kv_heads = nx
     parts = ny // kv_heads
+    y_heads = nz // parts
     inv_root = 1.0 / math.sqrt(HEAD_SIZE)
-    qbuf, kvs, kvb, osend, obuf, qp = r["qbuf"], r["kvs"], r["kvb"], r["osend"], r["obuf"], r["qp"]
-    q_start, _, q_near, q_far = net.relay(qbuf, r["q_s"], r["q_z"], r["q_f"])
+    qbuf, kvs, kvb, osend, obuf = r["qbuf"], r["kvs"], r["kvb"], r["osend"], r["obuf"]
+    q_start, q_recv = net.gather("z", qbuf, r["q_s"])
     q_start()
     for i in range(rows):
-        kvs[i] = kv[i:i + 1, :]
+        kvs[i] = qkv[i:i + 1, :]
 
     def place(i):
         return lax.rem(i, parts) * kv_heads + i // parts
@@ -339,48 +362,90 @@
     target, source = iota((count, count), 0), iota((count, count), 1)
     perm = one_hot(source == (target & 7) * rows + (target >> 3))
     lanes = iota((count, 128), 1)
-    shift = (gy & 15) * 8
-
-    def out_copy(head, agent, row, column):
+    shift = z * 8
+
+    def out_copy(head, t, agent, sent):
+        arrived = r["o_r"].at[jnp.where(head == gx, nx + z, gx)]
         return pltpu.make_async_remote_copy(
-            src_ref=osend.at[head, agent, pl.ds(0, 10)], dst_ref=obuf.at[row, column, pl.ds(0, 10)],
-            send_sem=r["o_s"].at[head], recv_sem=r["o_r"].at[row],
-            device_id=(head, agent), device_id_type=MESH)
-
-    def one_head(h):
-        columns = pl.ds(pl.multiple_of(h * 128, 128), 128)
-        blocks = [qbuf[h * parts + j, :, t * 128:(t + 1) * 128] for j in range(parts) for t in range(2)]
-        qh = dot(perm, jnp.concatenate(blocks, axis=0))
-        qp[h] = qh.reshape(rows, 8, 128)
-        scores = dot_t(qh.astype(BF16), r["pk_v"][:, columns]) * inv_root
+            src_ref=osend.at[t, agent, pl.ds(0, 10)], dst_ref=obuf.at[gx, z, pl.ds(0, 10)],
+            send_sem=r["o_s"].at[sent], recv_sem=arrived, device_id=(head, agent), device_id_type=MESH)
+
+    def one_head(t):
+        h = y * y_heads + t
+        blocks = [qbuf[t * parts + j, :, k * 128:(k + 1) * 128] for j in range(parts) for k in range(2)]
+        qh = dot(perm, jnp.concatenate(blocks, axis=0)).astype(BF16)
+        keys = r["pk_all"][:, :, t * 128:(t + 1) * 128].reshape(-1, 128)
+        scores = dot_t(qh, keys) * inv_root
         peak = jnp.max(scores, axis=1, keepdims=True)
         weights = jnp.exp(scores - peak)
         mass = jnp.sum(weights, axis=1, keepdims=True)
-        out = dot(weights.astype(BF16), r["pv_v"][:, columns]) / mass
-        osend[h, :, 0:8, :] = out.reshape(rows, 8, 128).astype(BF16)
+        if t == 0:
+            swaps[1][1]()
+        values = r["pv_all"][:, :, t * 128:(t + 1) * 128].reshape(-1, 128)
+        out = dot(weights.astype(BF16), values) / mass
+        osend[t, :, 0:8, :] = out.reshape(rows, 8, 128).astype(BF16)
         coded = coded_stats(peak, mass, lanes, shift).reshape(rows, 8, 128)
         line = jnp.sum(coded, axis=1, keepdims=True)
-        osend[h, :, 8:10, :] = jnp.broadcast_to(line, (rows, 2, 128)).astype(BF16)
+        osend[t, :, 8:10, :] = jnp.broadcast_to(line, (rows, 2, 128)).astype(BF16)
+
+        def own(s, c):
+            out_copy(h, t, gy, y_heads + t).start()
+            return c
 
         def send(s, c):
-            out_copy(h, lax.rem(gy + s, ny), gx, gy).start()
+            out_copy(h, t, lax.rem(gy + s, ny), t).start()
             return c
 
-        lax.fori_loop(jnp.where(h == gx, 1, 0), ny, send, 0)
-
-    for name in ("pk", "pv"):
-        load(name)
-    nz = net.nz
-    y_count, y = ny // nz, gy // nz
-    y_heads = nz // parts
-    q_near()
-    for t in [0] + sorted(range(1, y_count), key=lambda d: min(d, y_count - d)):
-        other = lax.rem(y + t, y_count)
-        if t:
-            q_far(other)
-        for i in range(y_heads):
-            one_head(other * y_heads + i)
-    obuf[gx, gy, 0:10, :] = osend[gx, gy, 0:10, :]
+        lax.fori_loop(jnp.where(h == gx, 1, 0), 1, own, 0)
+        lax.fori_loop(1, ny, send, 0)
+
+    def o_send():
+        for t in range(y_heads):
+            part = osend.at[t, pl.ds(0, ny - 1), pl.ds(0, 10)]
+            pltpu.make_async_remote_copy(
+                src_ref=part, dst_ref=part, send_sem=r["o_s"].at[t], recv_sem=r["o_r"].at[0],
+                device_id=(gx, lax.rem(gy + 1, ny)), device_id_type=MESH).wait_send()
+
+            def own(s, c):
+                out_copy(y * y_heads + t, t, gy, y_heads + t).wait_send()
+                return c
+
+            lax.fori_loop(jnp.where(y * y_heads + t == gx, 1, 0), 1, own, 0)
+
+    def o_recv():
+        for t in range(1, nx):
+            row = lax.rem(gx + t, nx)
+            part = obuf.at[row, :, pl.ds(0, 10)]
+            pltpu.make_async_remote_copy(
+                src_ref=part, dst_ref=part, send_sem=r["o_s"].at[0], recv_sem=r["o_r"].at[row],
+                device_id=(gx, lax.rem(gy + 1, ny)), device_id_type=MESH).wait_recv()
+
+        def own(s, c):
+            other = lax.rem(z + s, nz)
+            part = obuf.at[gx, other, pl.ds(0, 10)]
+            pltpu.make_async_remote_copy(
+                src_ref=part, dst_ref=part, send_sem=r["o_s"].at[0], recv_sem=r["o_r"].at[nx + other],
+                device_id=(gx, lax.rem(gy + 1, ny)), device_id_type=MESH).wait_recv()
+            return c
+
+        lax.fori_loop(jnp.where(gx // y_heads == y, 1, 0), nz, own, 0)
+
+    o_start, o_recv = net.phase(lambda: None, o_recv, o_send)
+    o_start()
+    width = y_heads * 128
+    own_columns = pl.ds(pl.multiple_of(y * width, 128), width)
+    r["pk_all"][y] = r["pk_v"][:, own_columns]
+    r["pv_all"][y] = r["pv_v"][:, own_columns]
+    q_recv()
+    swaps[0][1]()
+    for t in range(y_heads):
+        one_head(t)
+
+    def keep(s, c):
+        obuf[gx, z, 0:10, :] = osend[lax.rem(gx, y_heads), gy, 0:10, :]
+        return c
+
+    lax.fori_loop(jnp.where(gx // y_heads == y, 0, 1), 1, keep, 0)
     k_recv()
     head_row = iota((kv_heads, 128), 0)
     head_lane = iota((kv_heads, 128), 1)
@@ -389,7 +454,7 @@
     for p in range(parts):
         piece = jnp.zeros((kv_heads, 128), F32)
         for h in range(kv_heads):
-            piece = jnp.where(head_row == h, kvb[p * kv_heads + h], piece)
+            piece = jnp.where(head_row == h, kvb[p * kv_heads + h, :, 256:384], piece)
         here = (head_lane >> 5) == p
         new_k = jnp.where(here, pltpu.roll(piece, (32 * p - 64) % 128, 1), new_k)
         new_v = jnp.where(here, pltpu.roll(piece, (32 * p - 96) % 128, 1), new_v)
@@ -405,9 +470,13 @@
     span = r["sk_v"].shape[1]
     live = iota((8, span), 1) < r["len"][0]
     lane = iota((8, 128), 1)
+    row8 = iota((8, 128), 0)
     ss, sb = r["ss"], r["sb"]
     for h in range(kv_heads):
-        q_own = qp[h, gy]
+        q_own = jnp.zeros((8, 128), F32)
+        for g in range(8):
+            line = kvb[(g // 2) * kv_heads + h, :, (g % 2) * 128:(g % 2 + 1) * 128]
+            q_own = jnp.where(row8 == g, line, q_own)
         scores = dot_t(q_own.astype(BF16), r["sk_v"][0, :, h * 128:(h + 1) * 128]) * inv_root
         scores = jnp.where(live, scores, NEG)
         new_score = jnp.sum(q_own * new_k[h:h + 1, :], axis=1, keepdims=True) * inv_root
@@ -425,75 +494,46 @@
         ss.at[pl.ds(0, nx - 1), pl.ds(0, 10)], sb.at[pl.ds(0, nx - 1), pl.ds(0, 10)])
     s_start()
 
-    def out_all(ref, t, own_row):
-        row = lax.rem(gx + t, nx)
-        span_rows = ref.at[row, pl.ds(0, ny - 1 if t == 0 else ny), pl.ds(0, 10)]
-        return pltpu.make_async_remote_copy(
-            src_ref=span_rows, dst_ref=span_rows, send_sem=r["o_s"].at[row], recv_sem=r["o_r"].at[row],
-            device_id=(gx, lax.rem(gy + 1, ny)), device_id_type=MESH)
-
-    def o_recv():
-        for t in range(nx):
-            out_all(obuf, t, 0).wait_recv()
-
-    def o_send():
-        for t in range(nx):
-            out_all(osend, t, 0).wait_send()
-
-    o_start, o_recv = net.phase(lambda: None, o_recv, o_send)
-    o_start()
     s_recv()
     o_recv()
     sub = iota((8, 128), 0)
-    line_row, line_lane = iota((ny, 128), 0), iota((ny, 128), 1)
+    line_row, line_lane = iota((nz, 128), 0), iota((nz, 128), 1)
     here = (line_lane >> 3) == (line_row & 15)
     zero = jnp.zeros((nx, 128), F32)
-    halves = max(1, ny // 16)
-    size = ny // halves
     agent_row = iota((nx, 128), 0)
-    peaks, masses = [jnp.full((nx, 128), NEG, F32)] * halves, [zero] * halves
+    peaks, masses = zero, zero
     own = zero
     for i in range(nx):
         coded = obuf[i, :, 8:10, :].astype(F32)[:, 0, :]
         peak, mass = joined_stats(coded)
         peak, mass = jnp.where(here, peak, 0.0), jnp.where(here, mass, 0.0)
-        for k in range(halves):
-            part = slice(k * size, (k + 1) * size)
-            peaks[k] = jnp.where(agent_row == i, jnp.sum(peak[part], axis=0, keepdims=True), peaks[k])
-            masses[k] = jnp.where(agent_row == i, jnp.sum(mass[part], axis=0, keepdims=True), masses[k])
+        peaks = jnp.where(agent_row == i, jnp.sum(peak, axis=0, keepdims=True), peaks)
+        masses = jnp.where(agent_row == i, jnp.sum(mass, axis=0, keepdims=True), masses)
         own = jnp.where(agent_row == i, sb[i, 8:10, :].astype(F32)[0:1, :], own)
-    if size < 16:
-        there = iota((nx, 128), 1) < size * 8
-        peaks = [jnp.where(there, p, NEG) for p in peaks]
+    peaks = jnp.where(iota((nx, 128), 1) < nz * 8, peaks, NEG)
     own_peak, own_mass = joined_stats(own)
     first = iota((nx, 128), 1) < 8
     own_peak, own_mass = jnp.where(first, own_peak, 0.0), jnp.where(first, own_mass, 0.0)
     for step in (8, 16, 32, 64):
         own_peak = own_peak + pltpu.roll(own_peak, step, 1)
         own_mass = own_mass + pltpu.roll(own_mass, step, 1)
-    top = peaks[0]
-    for p in peaks[1:]:
-        top = jnp.maximum(top, p)
+    top = peaks
     for step in (8, 16, 32, 64):
         top = jnp.maximum(top, pltpu.roll(top, step, 1))
     top = jnp.maximum(top, own_peak)
-    shares = [m * jnp.exp(p - top) for m, p in zip(masses, peaks)]
+    share = masses * jnp.exp(peaks - top)
     own_share = own_mass * jnp.exp(own_peak - top)
-    whole = shares[0]
-    for share in shares[1:]:
-        whole = whole + share
+    whole = share
     for step in (8, 16, 32, 64):
         whole = whole + pltpu.roll(whole, step, 1)
     inverse = 1.0 / (whole + own_share)
     diagonal = (lane & 7) == sub
     att = r["att"]
     for i in range(nx):
-        wide = jnp.concatenate(
-            [jnp.where(diagonal, share[i:i + 1, :] * inverse[i:i + 1, :], 0.0) for share in shares], axis=1)
-        wide = wide[:, 0:ny * 8]
+        wide = jnp.where(diagonal, share[i:i + 1, :] * inverse[i:i + 1, :], 0.0)[:, 0:nz * 8]
         high = wide.astype(BF16)
         both = jnp.concatenate([high.astype(F32), wide - high.astype(F32)], axis=0).astype(BF16)
-        values = obuf[i, :, 0:8, :].astype(F32).reshape(ny * 8, 128).astype(BF16)
+        values = obuf[i, :, 0:8, :].astype(F32).reshape(nz * 8, 128).astype(BF16)
         mixed = dot(both, values)
         column = jnp.sum(jnp.where(lane == sub, own_share[i:i + 1, :] * inverse[i:i + 1, :], 0.0),
                          axis=1, keepdims=True)
@@ -575,6 +615,7 @@
     def local(tokens, norm_gain, query_matrix, key_matrix, value_matrix, output_matrix, adapter_down,
               query_lift, key_value_lift, mixer_down, mixer_lift, adapter_index, suffix_lengths,
               shared_prefix_keys, shared_prefix_values, private_suffix_keys, private_suffix_values):
+        block, heads = shared_prefix_keys.shape[0], nx // (ny // nz)
         arrays = dict(
             tokens=tokens, ml_in=mixer_lift.reshape(128, 256), ql=query_lift.reshape(128, 256), kvl=key_value_lift,
             idx=adapter_index.reshape(1, agents), down=adapter_down.transpose(0, 2, 1), kt=key_matrix.T,
@@ -587,19 +628,20 @@
             ("cs", (8, 128), F32), ("wc", (256, 1024), BF16), ("md", (128, 1024), BF16),
             ("rl_src", (nx, rows // 2, 128), F32), ("rl", (nx, rows // 2, 128), F32),
             ("rm_src", (nx, rows, 384), F32), ("rm", (nx, rows, 384), F32), ("al", (ny, rows // 2, 128), BF16),
-            ("qbuf", (ny, rows, 256), BF16), ("kvs", (rows, 1, 128), F32), ("kvb", (rows, 1, 128), F32),
-            ("osend", (nx, rows, 16, 128), BF16), ("obuf", (nx, ny, 16, 128), BF16),
+            ("qbuf", (nz, rows, 256), BF16), ("kvs", (rows, 1, 384), F32), ("kvb", (rows, 1, 384), F32),
+            ("pk_all", (ny // nz, block, heads * 128), BF16), ("pv_all", (ny // nz, block, heads * 128), BF16),
+            ("osend", (heads, rows, 16, 128), BF16), ("obuf", (nx, nz, 16, 128), BF16),
             ("ss", (nx, 16, 128), BF16), ("sb", (nx, 16, 128), BF16),
-            ("qp", (nx, rows, 8, 128), F32), ("att", (nx, 8, 128), F32),
+            ("att", (nx, 8, 128), F32),
             ("arow", (ny, nx, 1024), BF16), ("ml", (nx, 128, 256), BF16),
             ("xl_src", (nx, rows // 4, 128), F32), ("xl", (nx, rows // 4, 128), F32),
             ("xm_src", (nx, rows, 256), F32), ("xm", (nx, rows, 256), F32), ("zl", (ny, rows // 4, 128), BF16),
             ("ys", (rows, 1, 256), F32), ("yb", (rows, 1, 256), F32)]})
-        phases = ["tok", "lift", "rl", "rm", "al", "q", "kv", "ss", "ar", "ml", "xl", "xm", "zl", "y"]
+        phases = ["tok", "lift", "rl", "rm", "al", "q", "kv", "ss", "ar", "pk", "pv", "ml", "xl", "xm", "zl", "y"]
         scratch.update({name + "_s": sem((2,)) for name in phases})
-        scratch.update({name + "_z": sem((nz,)) for name in ("tok", "q", "ar")})
-        scratch.update({name + "_f": sem((ny // nz,)) for name in ("tok", "q", "ar")})
-        scratch.update(o_s=sem((nx,)), o_r=sem((nx,)))
+        scratch.update({name + "_z": sem((nz,)) for name in ("tok", "ar")})
+        scratch.update({name + "_f": sem((ny // nz,)) for name in ("tok", "ar")})
+        scratch.update(o_s=sem((2 * heads,)), o_r=sem((nx + nz,)))
         scratch["loads"] = sem((len(arrays),))
         names, extra = list(arrays), list(scratch)
 
@@ -614,8 +656,8 @@
             load = lambda name: copies[name].wait()
             prepare(net, r, load)
             net.wait_all()
-            kv, ml_recv = project(net, r, load)
-            attend(net, r, load, kv)
+            qkv, ml_recv, swaps = project(net, r, load)
+            attend(net, r, load, qkv, swaps)
             project_out(net, r, load, ml_recv, r["y_out"])
             net.finish()
 

time: 98.9 us -> 96.9 us (0.980)
  Pallas kernels: 96.7 us -> 94.6 us
    pallas_call x1, Pallas kernels: 96.7 us -> 94.6 us  [local(): pl.pallas_call(kernel, out_shape=jax.ShapeDtypeStruct((1, ny * 256), BF16...]
where the time goes in v5:
time: 96.9 us; the launch traced here: 96.7 us
  Pallas kernels  94.6 us (98%)
  local copies, waits for them, and re-layouts  1.41 us (1%)
    pallas_call x1, Pallas kernels, local(): pl.pallas_call(kernel, out_shape=jax.ShapeDtypeStruct((1, ny * 256), BF16...  94.6 us

profile of v5, /device:TPU:1, one launch (start us, length us, event | category | flops | bytes accessed | tf_op | source)
XLA Modules:
  0.0 96.7 jit_solution(15577212217346908854)
XLA Ops:
  0.7 94.6 %shard_map.163 = bf16[1,8192]{1,0:T(2,128)(2,1)} custom-call(bf16[8,1024]{1,0:T(8,128)(2,1)} %refs_0_.1, bf16[128,256]{1,0:T(8,128)(2,1)} %bitcast.9, bf16[128,256]{1,0:T(8,128)(2,1)} %bitcast.10, bf16[8,2,16,32]{3,2,1,0:T(8,128)(2,1)} %refs_3_.1, s32[1,256]{1,0:T(1,128)} %bitcast.15, bf16[2,48,1024]{2,1,0:T(8,128)(2,1)} %bitcast.8, ...), custom_call_target="tpu_custom_call" | custom-call | tf_op jit(solution)/shard_map/pallas_call | solution.py:665
  95.3 1.4 %copy.20 = bf16[1,8192]{1,0:T(2,128)(2,1)} copy(bf16[1,8192]{1,0:T(2,128)(2,1)} %shard_map.163) | data formatting | bytes 32768

commit v6 on v5

--- a/solution.py
+++ b/solution.py
@@ -43,6 +43,7 @@
         self.gx, self.gy = lax.axis_index("gx"), lax.axis_index("gy")
         self.nz = min(8, gy_count // 2)
         self.y, self.z = self.gy // self.nz, lax.rem(self.gy, self.nz)
+        self.x, self.core = self.gx // 2, lax.rem(self.gx, 2)
         self.phases = []
 
     def phase(self, start, wait_recv, wait_send):
@@ -234,7 +235,7 @@
     source, target = r[name + "_v"], r[name + "_all"]
     width = target.shape[2]
     count = target.shape[0]
-    columns = lambda i: pl.ds(pl.multiple_of(i * width, 128), width)
+    columns = lambda i: pl.ds(pl.multiple_of((i * 2 + net.core) * width, 128), width)
     part = target.at[pl.ds(0, count - 1)]
     return net.exchange("y", lambda p: source.at[:, columns(p)], lambda i: target.at[i], r[name + "_s"], part, part)
 
@@ -251,10 +252,10 @@
     load("wq")
     for name in ("pk", "pv"):
         load(name)
+    swaps = [swap_blocks(net, r, name) for name in ("pk", "pv")]
+    swaps[0][0]()
     t_recv()
-    swaps = [swap_blocks(net, r, name) for name in ("pk", "pv")]
-    for swap_start, _ in swaps:
-        swap_start()
+    swaps[1][0]()
     adapters = r["cols"][:, 0:1]
     x = tok[:, :, 0:1024].astype(F32).reshape(agents, 1024)
     scaled = (x * r["gain_v"][...]).astype(BF16)
@@ -310,12 +311,11 @@
     q = (summed[:, 0:256] + ADAPTER_SCALE * q_up) * factor
     kv_up = jnp.where(iota((rows, 128), 1) < 96, k_up, v_up)
     kv = (summed[:, 256:384] + ADAPTER_SCALE * kv_up) * factor
-    qbuf = r["qbuf"]
     heads = []
     for t in range(2):
         u = q[:, t * 128:(t + 1) * 128]
         heads.append((u * cosines + pltpu.roll(u, 64, 1) * sines).astype(BF16))
-        qbuf[net.z, :, t * 128:(t + 1) * 128] = heads[t]
+        r["qown"][:, t * 128:(t + 1) * 128] = heads[t]
     return jnp.concatenate([h.astype(F32) for h in heads] + [kv], axis=1), ml_recv, swaps
 
 
@@ -343,10 +343,57 @@
     rows = ny
     kv_heads = nx
     parts = ny // kv_heads
-    y_heads = nz // parts
+    assert nz == 2 * parts
+    x, core = net.x, net.core
     inv_root = 1.0 / math.sqrt(HEAD_SIZE)
     qbuf, kvs, kvb, osend, obuf = r["qbuf"], r["kvs"], r["kvb"], r["osend"], r["obuf"]
-    q_start, q_recv = net.gather("z", qbuf, r["q_s"])
+    q_core, q_part = z // parts, lax.rem(z, parts)
+    q_same = q_core == core
+
+    def q_copy(s):
+        arrived = r["q_r"].at[jnp.where(q_same, q_part, parts)]
+        return pltpu.make_async_remote_copy(
+            src_ref=r["qown"], dst_ref=qbuf.at[core * parts + q_part], send_sem=r["q_s"].at[jnp.minimum(s, 1)],
+            recv_sem=arrived, device_id=(x * 2 + q_core, y * nz + lax.rem(z + s, nz)), device_id_type=MESH)
+
+    def q_wait(part, sent, arrived):
+        return pltpu.make_async_remote_copy(
+            src_ref=part, dst_ref=part, send_sem=r["q_s"].at[sent], recv_sem=r["q_r"].at[arrived],
+            device_id=(gx, y * nz + lax.rem(z + 1, nz)), device_id_type=MESH)
+
+    def q_begin():
+        def one(s, c):
+            q_copy(s).start()
+            return c
+
+        lax.fori_loop(jnp.where(q_same, 1, 0), nz, one, 0)
+
+        def keep(s, c):
+            qbuf[core * parts + q_part] = r["qown"][...]
+            return c
+
+        lax.fori_loop(jnp.where(q_same, 0, 1), 1, keep, 0)
+
+    def q_receive():
+        q_wait(qbuf.at[pl.ds((1 - core) * parts, parts)], 0, parts).wait_recv()
+
+        def one(s, c):
+            other = lax.rem(z + s, parts)
+            q_wait(qbuf.at[core * parts + other], 0, other).wait_recv()
+            return c
+
+        lax.fori_loop(jnp.where(q_same, 1, 0), parts, one, 0)
+
+    def q_sent():
+        q_wait(qbuf.at[pl.ds(0, nz - 1)], 1, 0).wait_send()
+
+        def one(s, c):
+            q_copy(s).wait_send()
+            return c
+
+        lax.fori_loop(jnp.where(q_same, 1, 0), 1, one, 0)
+
+    q_start, q_recv = net.phase(q_begin, q_receive, q_sent)
     q_start()
     for i in range(rows):
         kvs[i] = qkv[i:i + 1, :]
@@ -364,88 +411,86 @@
     lanes = iota((count, 128), 1)
     shift = z * 8
 
-    def out_copy(head, t, agent, sent):
-        arrived = r["o_r"].at[jnp.where(head == gx, nx + z, gx)]
+    h = y * 2 + core
+    mine = h == gx
+
+    def out_copy(k, agent, sent):
+        row = x * 2 + k
+        arrived = r["o_r"].at[jnp.where(h // 2 == x, nx + k * nz + z, row)]
         return pltpu.make_async_remote_copy(
-            src_ref=osend.at[t, agent, pl.ds(0, 10)], dst_ref=obuf.at[gx, z, pl.ds(0, 10)],
-            send_sem=r["o_s"].at[sent], recv_sem=arrived, device_id=(head, agent), device_id_type=MESH)
-
-    def one_head(t):
-        h = y * y_heads + t
-        blocks = [qbuf[t * parts + j, :, k * 128:(k + 1) * 128] for j in range(parts) for k in range(2)]
+            src_ref=osend.at[k, agent, pl.ds(0, 10)], dst_ref=obuf.at[row, z, pl.ds(0, 10)],
+            send_sem=r["o_s"].at[sent], recv_sem=arrived, device_id=(h, agent), device_id_type=MESH)
+
+    def out_wait(part, sent, arrived):
+        return pltpu.make_async_remote_copy(
+            src_ref=part, dst_ref=part, send_sem=r["o_s"].at[sent], recv_sem=r["o_r"].at[arrived],
+            device_id=(gx, lax.rem(gy + 1, ny)), device_id_type=MESH)
+
+    def one_row(k):
+        blocks = [qbuf[k * parts + j, :, t * 128:(t + 1) * 128] for j in range(parts) for t in range(2)]
         qh = dot(perm, jnp.concatenate(blocks, axis=0)).astype(BF16)
-        keys = r["pk_all"][:, :, t * 128:(t + 1) * 128].reshape(-1, 128)
-        scores = dot_t(qh, keys) * inv_root
+        scores = dot_t(qh, r["pk_all"][...].reshape(-1, 128)) * inv_root
         peak = jnp.max(scores, axis=1, keepdims=True)
         weights = jnp.exp(scores - peak)
         mass = jnp.sum(weights, axis=1, keepdims=True)
-        if t == 0:
+        if k == 0:
             swaps[1][1]()
-        values = r["pv_all"][:, :, t * 128:(t + 1) * 128].reshape(-1, 128)
-        out = dot(weights.astype(BF16), values) / mass
-        osend[t, :, 0:8, :] = out.reshape(rows, 8, 128).astype(BF16)
+        out = dot(weights.astype(BF16), r["pv_all"][...].reshape(-1, 128)) / mass
+        osend[k, :, 0:8, :] = out.reshape(rows, 8, 128).astype(BF16)
         coded = coded_stats(peak, mass, lanes, shift).reshape(rows, 8, 128)
         line = jnp.sum(coded, axis=1, keepdims=True)
-        osend[t, :, 8:10, :] = jnp.broadcast_to(line, (rows, 2, 128)).astype(BF16)
+        osend[k, :, 8:10, :] = jnp.broadcast_to(line, (rows, 2, 128)).astype(BF16)
 
         def own(s, c):
-            out_copy(h, t, gy, y_heads + t).start()
+            out_copy(k, gy, 2 + k).start()
             return c
 
         def send(s, c):
-            out_copy(h, t, lax.rem(gy + s, ny), t).start()
+            out_copy(k, lax.rem(gy + s, ny), k).start()
             return c
 
-        lax.fori_loop(jnp.where(h == gx, 1, 0), 1, own, 0)
+        lax.fori_loop(jnp.where(mine, 1, 0), 1, own, 0)
         lax.fori_loop(1, ny, send, 0)
 
     def o_send():
-        for t in range(y_heads):
-            part = osend.at[t, pl.ds(0, ny - 1), pl.ds(0, 10)]
-            pltpu.make_async_remote_copy(
-                src_ref=part, dst_ref=part, send_sem=r["o_s"].at[t], recv_sem=r["o_r"].at[0],
-                device_id=(gx, lax.rem(gy + 1, ny)), device_id_type=MESH).wait_send()
+        for k in range(2):
+            out_wait(osend.at[k, pl.ds(0, ny - 1), pl.ds(0, 10)], k, 0).wait_send()
 
             def own(s, c):
-                out_copy(y * y_heads + t, t, gy, y_heads + t).wait_send()
+                out_copy(k, gy, 2 + k).wait_send()
                 return c
 
-            lax.fori_loop(jnp.where(y * y_heads + t == gx, 1, 0), 1, own, 0)
+            lax.fori_loop(jnp.where(mine, 1, 0), 1, own, 0)
 
     def o_recv():
-        for t in range(1, nx):
-            row = lax.rem(gx + t, nx)
-            part = obuf.at[row, :, pl.ds(0, 10)]
-            pltpu.make_async_remote_copy(
-                src_ref=part, dst_ref=part, send_sem=r["o_s"].at[0], recv_sem=r["o_r"].at[row],
-                device_id=(gx, lax.rem(gy + 1, ny)), device_id_type=MESH).wait_recv()
-
-        def own(s, c):
-            other = lax.rem(z + s, nz)
-            part = obuf.at[gx, other, pl.ds(0, 10)]
-            pltpu.make_async_remote_copy(
-                src_ref=part, dst_ref=part, send_sem=r["o_s"].at[0], recv_sem=r["o_r"].at[nx + other],
-                device_id=(gx, lax.rem(gy + 1, ny)), device_id_type=MESH).wait_recv()
-            return c
-
-        lax.fori_loop(jnp.where(gx // y_heads == y, 1, 0), nz, own, 0)
+        for k in range(2):
+            for t in range(1, nx // 2):
+                row = lax.rem(x + t, nx // 2) * 2 + k
+                out_wait(obuf.at[row, :, pl.ds(0, 10)], 0, row).wait_recv()
+
+            def own(s, c):
+                other = lax.rem(z + s, nz)
+                out_wait(obuf.at[x * 2 + k, other, pl.ds(0, 10)], 0, nx + k * nz + other).wait_recv()
+                return c
+
+            lax.fori_loop(jnp.where(x == y, 1, 0), nz, own, 0)
 
     o_start, o_recv = net.phase(lambda: None, o_recv, o_send)
     o_start()
-    width = y_heads * 128
-    own_columns = pl.ds(pl.multiple_of(y * width, 128), width)
+    own_columns = pl.ds(pl.multiple_of(h * 128, 128), 128)
     r["pk_all"][y] = r["pk_v"][:, own_columns]
     r["pv_all"][y] = r["pv_v"][:, own_columns]
     q_recv()
     swaps[0][1]()
-    for t in range(y_heads):
-        one_head(t)
+    for k in range(2):
+        one_row(k)
 
     def keep(s, c):
-        obuf[gx, z, 0:10, :] = osend[lax.rem(gx, y_heads), gy, 0:10, :]
+        for k in range(2):
+            obuf[x * 2 + k, z, 0:10, :] = osend[k, gy, 0:10, :]
         return c
 
-    lax.fori_loop(jnp.where(gx // y_heads == y, 0, 1), 1, keep, 0)
+    lax.fori_loop(jnp.where(mine, 0, 1), 1, keep, 0)
     k_recv()
     head_row = iota((kv_heads, 128), 0)
     head_lane = iota((kv_heads, 128), 1)
@@ -615,7 +660,7 @@
     def local(tokens, norm_gain, query_matrix, key_matrix, value_matrix, output_matrix, adapter_down,
               query_lift, key_value_lift, mixer_down, mixer_lift, adapter_index, suffix_lengths,
               shared_prefix_keys, shared_prefix_values, private_suffix_keys, private_suffix_values):
-        block, heads = shared_prefix_keys.shape[0], nx // (ny // nz)
+        block = shared_prefix_keys.shape[0]
         arrays = dict(
             tokens=tokens, ml_in=mixer_lift.reshape(128, 256), ql=query_lift.reshape(128, 256), kvl=key_value_lift,
             idx=adapter_index.reshape(1, agents), down=adapter_down.transpose(0, 2, 1), kt=key_matrix.T,
@@ -628,9 +673,9 @@
             ("cs", (8, 128), F32), ("wc", (256, 1024), BF16), ("md", (128, 1024), BF16),
             ("rl_src", (nx, rows // 2, 128), F32), ("rl", (nx, rows // 2, 128), F32),
             ("rm_src", (nx, rows, 384), F32), ("rm", (nx, rows, 384), F32), ("al", (ny, rows // 2, 128), BF16),
-            ("qbuf", (nz, rows, 256), BF16), ("kvs", (rows, 1, 384), F32), ("kvb", (rows, 1, 384), F32),
-            ("pk_all", (ny // nz, block, heads * 128), BF16), ("pv_all", (ny // nz, block, heads * 128), BF16),
-            ("osend", (heads, rows, 16, 128), BF16), ("obuf", (nx, nz, 16, 128), BF16),
+            ("qbuf", (nz, rows, 256), BF16), ("qown", (rows, 256), BF16), ("kvs", (rows, 1, 384), F32), ("kvb", (rows, 1, 384), F32),
+            ("pk_all", (ny // nz, block, 128), BF16), ("pv_all", (ny // nz, block, 128), BF16),
+            ("osend", (2, rows, 16, 128), BF16), ("obuf", (nx, nz, 16, 128), BF16),
             ("ss", (nx, 16, 128), BF16), ("sb", (nx, 16, 128), BF16),
             ("att", (nx, 8, 128), F32),
             ("arow", (ny, nx, 1024), BF16), ("ml", (nx, 128, 256), BF16),
@@ -641,7 +686,7 @@
         scratch.update({name + "_s": sem((2,)) for name in phases})
         scratch.update({name + "_z": sem((nz,)) for name in ("tok", "ar")})
         scratch.update({name + "_f": sem((ny // nz,)) for name in ("tok", "ar")})
-        scratch.update(o_s=sem((2 * heads,)), o_r=sem((nx + nz,)))
+        scratch.update(o_s=sem((4,)), o_r=sem((nx + 2 * nz,)), q_r=sem((nz,)))
         scratch["loads"] = sem((len(arrays),))
         names, extra = list(arrays), list(scratch)
 

time: 96.9 us -> 86.3 us (0.89)
  Pallas kernels: 94.6 us -> 84 us
    pallas_call x1, Pallas kernels: 94.6 us -> 84 us  [local(): pl.pallas_call(kernel, out_shape=jax.ShapeDtypeStruct((1, ny * 256), BF16...]
where the time goes in v6:
time: 86.3 us; the launch traced here: 86.1 us
  Pallas kernels  84 us (97%)
  local copies, waits for them, and re-layouts  1.41 us (2%)
    pallas_call x1, Pallas kernels, local(): pl.pallas_call(kernel, out_shape=jax.ShapeDtypeStruct((1, ny * 256), BF16...  84 us

profile of v6, /device:TPU:1, one launch (start us, length us, event | category | flops | bytes accessed | tf_op | source)
XLA Modules:
  0.0 86.1 jit_solution(18141894861205576084)
XLA Ops:
  0.7 84.0 %shard_map.163 = bf16[1,8192]{1,0:T(2,128)(2,1)} custom-call(bf16[8,1024]{1,0:T(8,128)(2,1)} %refs_0_.1, bf16[128,256]{1,0:T(8,128)(2,1)} %bitcast.9, bf16[128,256]{1,0:T(8,128)(2,1)} %bitcast.10, bf16[8,2,16,32]{3,2,1,0:T(8,128)(2,1)} %refs_3_.1, s32[1,256]{1,0:T(1,128)} %bitcast.15, bf16[2,48,1024]{2,1,0:T(8,128)(2,1)} %bitcast.8, ...), custom_call_target="tpu_custom_call" | custom-call | tf_op jit(solution)/shard_map/pallas_call | solution.py:710
  84.6 1.4 %copy.20 = bf16[1,8192]{1,0:T(2,128)(2,1)} copy(bf16[1,8192]{1,0:T(2,128)(2,1)} %shard_map.163) | data formatting | bytes 32768

commit v7 on v6

--- a/solution.py
+++ b/solution.py
@@ -253,9 +253,8 @@
     for name in ("pk", "pv"):
         load(name)
     swaps = [swap_blocks(net, r, name) for name in ("pk", "pv")]
+    t_recv()
     swaps[0][0]()
-    t_recv()
-    swaps[1][0]()
     adapters = r["cols"][:, 0:1]
     x = tok[:, :, 0:1024].astype(F32).reshape(agents, 1024)
     scaled = (x * r["gain_v"][...]).astype(BF16)
@@ -302,6 +301,7 @@
     ml_start()
     lift_all = lift[...].reshape(width, 384)
     al_recv()
+    swaps[1][0]()
     packed = jnp.sum(al[...].astype(F32), axis=0)
     lowrank = jnp.concatenate([packed, pltpu.roll(packed, 64, 1)], axis=0)
     lowrank = jnp.where(iota((rows, 128), 1) < 3 * RANK, lowrank, 0.0).astype(BF16)

time: 86.3 us -> 85.2 us (0.987)
  Pallas kernels: 84 us -> 83 us
    pallas_call x1, Pallas kernels: 84 us -> 83 us  [local(): pl.pallas_call(kernel, out_shape=jax.ShapeDtypeStruct((1, ny * 256), BF16...]
where the time goes in v7:
time: 85.2 us; the launch traced here: 85.1 us
  Pallas kernels  83 us (97%)
  local copies, waits for them, and re-layouts  1.41 us (2%)
    pallas_call x1, Pallas kernels, local(): pl.pallas_call(kernel, out_shape=jax.ShapeDtypeStruct((1, ny * 256), BF16...  83 us

profile of v7, /device:TPU:1, one launch (start us, length us, event | category | flops | bytes accessed | tf_op | source)
XLA Modules:
  0.0 85.1 jit_solution(1903289747004901715)
XLA Ops:
  0.7 83.0 %shard_map.163 = bf16[1,8192]{1,0:T(2,128)(2,1)} custom-call(bf16[8,1024]{1,0:T(8,128)(2,1)} %refs_0_.1, bf16[128,256]{1,0:T(8,128)(2,1)} %bitcast.9, bf16[128,256]{1,0:T(8,128)(2,1)} %bitcast.10, bf16[8,2,16,32]{3,2,1,0:T(8,128)(2,1)} %refs_3_.1, s32[1,256]{1,0:T(1,128)} %bitcast.15, bf16[2,48,1024]{2,1,0:T(8,128)(2,1)} %bitcast.8, ...), custom_call_target="tpu_custom_call" | custom-call | tf_op jit(solution)/shard_map/pallas_call | solution.py:710
  83.7 1.4 %copy.20 = bf16[1,8192]{1,0:T(2,128)(2,1)} copy(bf16[1,8192]{1,0:T(2,128)(2,1)} %shard_map.163) | data formatting | bytes 32768
